TPU v7x, 256 devices: a whole 4x4x8 slice. The times are simulated.
256 devices in a mesh: req: 32 (over x, y, core), kv: 8 (over z).
Axes of the slice: x: 4, y: 4, z: 8, core: 2. Of those that a mesh axis runs over, the one named last changes fastest.
Arguments:
- hidden_in: bfloat16 [256, 4096], P(None, 'req'), may hold values from -15 to 15
- norm_gain: bfloat16 [2, 4096], P(None, 'req'), may hold values from 0.5 to 1.5
- q_gain: bfloat16 [2, 128], replicated, may hold values from 0.25 to 1.75
- k_gain: bfloat16 [2, 128], replicated, may hold values from 0.25 to 1.75
- w_query: bfloat16 [2, 4096, 4096], P(None, 'req', 'kv'), may hold values from -0.09375 to 0.09375
- w_key: bfloat16 [2, 4096, 1024], P(None, 'req', 'kv'), may hold values from -0.09375 to 0.09375
- w_value: bfloat16 [2, 4096, 1024], P(None, 'req', 'kv'), may hold values from -0.09375 to 0.09375
- w_out: bfloat16 [2, 4096, 4096], P(None, 'kv', 'req'), may hold values from -0.09375 to 0.09375
- cache_keys: bfloat16 [2, 1536, 128, 1024], P(None, 'req', None, 'kv'), may hold values from -180 to 180
- cache_values: bfloat16 [2, 1536, 128, 1024], P(None, 'req', None, 'kv'), may hold values from -4 to 4
- lengths: int32 [256], replicated, may hold values from 1 to 16384, as said below
- block_owner: int32 [1536], P('req'), may hold values from 0 to 255, as said below
- block_fill: int32 [1536], P('req'), may hold values from 0 to 128
Outputs:
- hidden_out: bfloat16 [256, 4096], P(None, 'req')
- new_keys: bfloat16 [2, 256, 1024], P(None, 'req', 'kv')
- new_values: bfloat16 [2, 256, 1024], P(None, 'req', 'kv')
Inputs may be any that keep to these rules, and one draw needn't show every extreme that they name: `lengths`: the longest request has 16384 cached tokens. Exactly 4 requests have more than 128 cached tokens. `block_owner`: request r owns block (r // 8) * 48 + r % 8, whose fill is above 0; its other blocks lie anywhere among the remaining blocks of the pool. The fills of the blocks owned by r sum to lengths[r], and all of them but at most one are 128. A block with fill 0 holds nothing, whatever its owner.
All inputs are finite; a program needn't handle non-finite values.
Results may differ from a plain program's by a relative error of at most 0.024.
Values may be sent and summed in bfloat16 or wider, within the bound.
A program may use at most 64 MiB of HBM per device.

v0:
```python
import math

import jax
import jax.numpy as jnp
from jax import lax
from jax.sharding import PartitionSpec as P

D = 4096
LAYERS = 2


EPS = 1e-06
THETA = 1000000.0
FLOOR = -1e30


def joined(array, axis, combine):
    everything = jax.tree.map(lambda part: lax.all_gather(part, axis), array)
    first = jax.tree.map(lambda part: part[0], everything)

    def step(k, so_far):
        return combine(so_far, jax.tree.map(lambda part: part[k], everything))

    return lax.fori_loop(1, lax.axis_size(axis), step, first)


def head_norm_rope(values, head_gain, positions, head_dim):
    row_count = values.shape[0]
    head_count = values.shape[1] // head_dim
    pieces = values.reshape(row_count, head_count, head_dim)
    pieces = (
        pieces
        * lax.rsqrt(jnp.mean(pieces * pieces, axis=2, keepdims=True) + EPS)
        * head_gain.astype(jnp.float32)
    )
    half_dim = head_dim // 2
    frequency = THETA ** (-(jnp.arange(half_dim, dtype=jnp.float32) * 2.0 / head_dim))
    angles = positions.astype(jnp.float32)[:, None] * frequency[None, :]
    cosine = jnp.cos(angles)[:, None, :]
    sine_part = jnp.sin(angles)[:, None, :]
    lower_half = pieces[:, :, :half_dim]
    upper_half = pieces[:, :, half_dim:]
    turned = jnp.concatenate(
        [
            lower_half * cosine - upper_half * sine_part,
            upper_half * cosine + lower_half * sine_part,
        ],
        axis=2,
    )
    return turned.reshape(row_count, head_count * head_dim).astype(jnp.bfloat16)


def join_partials(first_part, other_part):
    first_max, first_den, first_num = first_part
    other_max, other_den, other_num = other_part
    joint_max = jnp.maximum(first_max, other_max)
    first_scale = jnp.exp(first_max - joint_max)
    other_scale = jnp.exp(other_max - joint_max)
    joint_den = first_den * first_scale + other_den * other_scale
    joint_num = first_num * first_scale[:, :, None] + other_num * other_scale[:, :, None]
    return (joint_max, joint_den, joint_num)


def on_device(
    hidden_in,
    norm_gain,
    q_gain,
    k_gain,
    w_query,
    w_key,
    w_value,
    w_out,
    cache_keys,
    cache_values,
    lengths,
    block_owner,
    block_fill,
):
    device_count = lax.axis_size("req")
    my_index = lax.axis_index("req")
    request_count = hidden_in.shape[0]
    own_rows = request_count // device_count
    head_dim = q_gain.shape[1]
    query_cols = w_query.shape[2]
    key_cols = w_key.shape[2]
    query_heads = query_cols // head_dim
    kv_heads = key_cols // head_dim
    group_size = query_heads // kv_heads
    slot_count = cache_keys.shape[1]
    block_len = cache_keys.shape[2]
    row_start = my_index * own_rows
    own_lengths = lax.dynamic_slice_in_dim(lengths, row_start, own_rows, 0)
    live_mask = (jnp.arange(block_len, dtype=jnp.int32)[None, :] < block_fill[:, None])[
        :, None, None, :
    ]
    logit_scale_factor = 1.0 / math.sqrt(head_dim)
    hidden = hidden_in
    key_list = []
    value_list = []
    for layer_index in range(LAYERS):
        wide = hidden.astype(jnp.float32)
        square_sum = lax.psum(jnp.sum(wide * wide, axis=1), "req")
        normed = (
            wide
            * lax.rsqrt(square_sum[:, None] / D + EPS)
            * norm_gain[layer_index].astype(jnp.float32)
        ).astype(jnp.bfloat16)
        w_joined = jnp.concatenate(
            [w_query[layer_index], w_key[layer_index], w_value[layer_index]], axis=1
        )
        summed = lax.psum(jnp.dot(normed, w_joined, preferred_element_type=jnp.float32), "req")
        all_queries = head_norm_rope(summed[:, :query_cols], q_gain[layer_index], lengths, head_dim)
        own_sums = lax.dynamic_slice_in_dim(summed, row_start, own_rows, 0)
        own_queries = lax.dynamic_slice_in_dim(all_queries, row_start, own_rows, 0)
        own_keys = head_norm_rope(
            own_sums[:, query_cols : query_cols + key_cols],
            k_gain[layer_index],
            own_lengths,
            head_dim,
        )
        own_values = own_sums[:, query_cols + key_cols :].astype(jnp.bfloat16)
        paged_key_rows = cache_keys[layer_index].reshape(slot_count, block_len, kv_heads, head_dim)
        paged_value_rows = cache_values[layer_index].reshape(
            slot_count, block_len, kv_heads, head_dim
        )
        selected_entry = all_queries[block_owner].reshape(
            slot_count, kv_heads, group_size, head_dim
        )
        attention_logits = (
            jnp.einsum(
                "bkhd,bhgd->bhgk",
                paged_key_rows,
                selected_entry,
                preferred_element_type=jnp.float32,
            )
            * logit_scale_factor
        )
        attention_logits = jnp.where(live_mask, attention_logits, -jnp.inf)
        block_max = jnp.maximum(jnp.max(attention_logits, axis=3), FLOOR)
        weights = jnp.where(live_mask, jnp.exp(attention_logits - block_max[:, :, :, None]), 0.0)
        block_den = jnp.sum(weights, axis=3)
        block_numerator = jnp.einsum(
            "bhgk,bkhd->bhgd",
            weights.astype(jnp.bfloat16),
            paged_value_rows,
            preferred_element_type=jnp.float32,
        )
        flat_max = block_max.reshape(slot_count, query_heads)
        local_max = jnp.maximum(
            jax.ops.segment_max(flat_max, block_owner, num_segments=request_count), FLOOR
        )
        factor = jnp.exp(flat_max - local_max[block_owner])
        local_den = jax.ops.segment_sum(
            factor * block_den.reshape(slot_count, query_heads),
            block_owner,
            num_segments=request_count,
        )
        local_num = jax.ops.segment_sum(
            factor[:, :, None] * block_numerator.reshape(slot_count, query_heads, head_dim),
            block_owner,
            num_segments=request_count,
        )
        query_own = own_queries.astype(jnp.float32).reshape(
            own_rows, kv_heads, group_size, head_dim
        )
        key_own = own_keys.astype(jnp.float32).reshape(own_rows, kv_heads, 1, head_dim)
        own_score = (
            jnp.sum(query_own * key_own, axis=3).reshape(own_rows, query_heads) * logit_scale_factor
        )
        value_own = jnp.broadcast_to(
            own_values.astype(jnp.float32).reshape(own_rows, kv_heads, 1, head_dim),
            (own_rows, kv_heads, group_size, head_dim),
        ).reshape(own_rows, query_heads, head_dim)
        prior_max = lax.dynamic_slice_in_dim(local_max, row_start, own_rows, 0)
        prior_den = lax.dynamic_slice_in_dim(local_den, row_start, own_rows, 0)
        prior_num = lax.dynamic_slice_in_dim(local_num, row_start, own_rows, 0)
        joint_max = jnp.maximum(prior_max, own_score)
        keep_scale = jnp.exp(prior_max - joint_max)
        fresh_scale = jnp.exp(own_score - joint_max)
        local_max = lax.dynamic_update_slice_in_dim(local_max, joint_max, row_start, 0)
        local_den = lax.dynamic_update_slice_in_dim(
            local_den, prior_den * keep_scale + fresh_scale, row_start, 0
        )
        local_num = lax.dynamic_update_slice_in_dim(
            local_num,
            prior_num * keep_scale[:, :, None] + fresh_scale[:, :, None] * value_own,
            row_start,
            0,
        )
        merged_max, merged_den, merged_num = joined(
            (local_max, local_den, local_num), "req", join_partials
        )
        attended = (
            (merged_num / merged_den[:, :, None])
            .reshape(request_count, query_cols)
            .astype(jnp.bfloat16)
        )
        partial_out = jnp.dot(attended, w_out[layer_index], preferred_element_type=jnp.float32)
        branch = lax.psum(partial_out, "kv")
        hidden = (wide + branch).astype(jnp.bfloat16)
        key_list.append(own_keys)
        value_list.append(own_values)
    return (hidden, jnp.stack(key_list), jnp.stack(value_list))


def solution(mesh):
    in_specs = (
        P(None, "req"),
        P(None, "req"),
        P(),
        P(),
        P(None, "req", "kv"),
        P(None, "req", "kv"),
        P(None, "req", "kv"),
        P(None, "kv", "req"),
        P(None, "req", None, "kv"),
        P(None, "req", None, "kv"),
        P(),
        P("req"),
        P("req"),
    )
    out_specs = (P(None, "req"), P(None, "req", "kv"), P(None, "req", "kv"))
    return jax.shard_map(
        on_device, mesh=mesh, in_specs=in_specs, out_specs=out_specs, check_vma=False
    )
```

profile of v0, /device:TPU:1, one launch (start us, length us, event | category | flops | bytes accessed | tf_op | source)
XLA Modules:
  0.0 872.4 jit_solution(6818904741598166862)
XLA Ops:
  9.9 65.3 %psum.42 = f32[256]{0:T(256)S(1)} all-reduce(f32[256]{0:T(256)S(1)} %fusion.56), channel_id=1, replica_groups=mesh['req'=32,'kv'=8] {'req'}, use_global_device_ids=true, to_apply=%region_1.0 | all-reduce | flops 256 | bytes 2048 | tf_op jit(solution)/shard_map/psum | solution.py:102
  76.0 2.0 fusion.44
  83.0 109.9 %all-reduce.5.cloned.1.call-done = f32[256,768]{1,0:T(8,128)} async-done(((f32[256,768]{1,0:T(8,128)}), f32[256,768]{1,0:T(8,128)}) %all-reduce.5.cloned.1.call-update) | async-done | bytes 786448 | tf_op jit(solution)/shard_map/psum | solution.py:111
  196.5 2.4 fusion.123
  200.5 2.0 fusion.26
  202.6 2.2 scatter_fusion
  209.5 25.6 %all_gather.53 = f32[32,256,4]{1,2,0:T(4,128)S(1)} all-gather(f32[1,256,4]{1,2,0:T(4,128)S(1)} %copy.132), channel_id=1, replica_groups=mesh['req'=32,'kv'=8] {'req'}, dimensions={0}, use_global_device_ids=true | all-gather | bytes 135168 | tf_op jit(solution)/shard_map/all_gather | solution.py:18
  235.1 21.9 %all_gather.50 = f32[32,256,4]{1,2,0:T(4,128)S(1)} all-gather(f32[1,256,4]{1,2,0:T(4,128)S(1)} %copy.129), channel_id=1, replica_groups=mesh['req'=32,'kv'=8] {'req'}, dimensions={0}, use_global_device_ids=true | all-gather | bytes 135168 | tf_op jit(solution)/shard_map/all_gather | solution.py:18
  257.0 30.1 %all-gather.3.cloned.1.call-done = f32[32,256,4,128]{3,1,2,0:T(8,128)} async-done(((f32[1,256,4,128]{3,1,2,0:T(8,128)}), f32[32,256,4,128]{3,1,2,0:T(8,128)}) %all-gather.3.cloned.1.call-update) | async-done | bytes 16777232 | tf_op jit(solution)/shard_map/all_gather | solution.py:18
  288.5 83.6 %while.38 = (s32[]{:T(128)}, f32[256,4]{0,1:T(4,128)S(1)}, f32[256,4]{0,1:T(4,128)S(1)}, f32[256,4,128]{2,1,0:T(4,128)S(1)}, f32[32,256,4]{1,2,0:T(4,128)S(1)}, ...) while((s32[]{:T(128)}, f32[256,4]{0,1:T(4,128)S(1)}, ...), condition=%wide.region_12.13_spmd, body=%wide.region_11.12_spmd.sunk | while | flops 399365 | bytes 2678935 | solution.py:24
  292.6 1.3 fusion.132
  295.3 1.3 fusion.132
  373.6 66.1 %all-reduce.7.cloned.1.call-done = f32[256,128]{1,0:T(8,128)} async-done(((f32[256,128]{1,0:T(8,128)}), f32[256,128]{1,0:T(8,128)}) %all-reduce.7.cloned.1.call-update) | async-done | bytes 131088 | tf_op jit(solution)/shard_map/psum | solution.py:199
  440.7 67.7 %psum.45 = f32[256]{0:T(256)S(1)} all-reduce(f32[256]{0:T(256)S(1)} %get-tuple-element.472), channel_id=1, replica_groups=mesh['req'=32,'kv'=8] {'req'}, use_global_device_ids=true, to_apply=%region_15.16 | all-reduce | flops 256 | bytes 2048 | tf_op jit(solution)/shard_map/psum | solution.py:102
  509.9 107.3 %all-reduce.9.cloned.1.call-done = f32[256,768]{1,0:T(8,128)} async-done(((f32[256,768]{1,0:T(8,128)}), f32[256,768]{1,0:T(8,128)}) %all-reduce.9.cloned.1.call-update) | async-done | bytes 786448 | tf_op jit(solution)/shard_map/psum | solution.py:111
  620.8 2.4 fusion.124
  624.8 2.0 fusion.35
  626.9 2.2 scatter_fusion.1
  633.8 25.6 %all_gather.62 = f32[32,256,4]{1,2,0:T(4,128)S(1)} all-gather(f32[1,256,4]{1,2,0:T(4,128)S(1)} %copy.145), channel_id=1, replica_groups=mesh['req'=32,'kv'=8] {'req'}, dimensions={0}, use_global_device_ids=true | all-gather | bytes 135168 | tf_op jit(solution)/shard_map/all_gather | solution.py:18
  659.4 21.9 %all_gather.59 = f32[32,256,4]{1,2,0:T(4,128)S(1)} all-gather(f32[1,256,4]{1,2,0:T(4,128)S(1)} %copy.142), channel_id=1, replica_groups=mesh['req'=32,'kv'=8] {'req'}, dimensions={0}, use_global_device_ids=true | all-gather | bytes 135168 | tf_op jit(solution)/shard_map/all_gather | solution.py:18
  681.3 30.1 %all-gather.5.cloned.1.call-done = f32[32,256,4,128]{3,1,2,0:T(8,128)} async-done(((f32[1,256,4,128]{3,1,2,0:T(8,128)}), f32[32,256,4,128]{3,1,2,0:T(8,128)}) %all-gather.5.cloned.1.call-update) | async-done | bytes 16777232 | tf_op jit(solution)/shard_map/all_gather | solution.py:18
  712.8 83.6 %while.39 = (s32[]{:T(128)}, f32[256,4]{0,1:T(4,128)S(1)}, f32[256,4]{0,1:T(4,128)S(1)}, f32[256,4,128]{2,1,0:T(4,128)S(1)}, f32[32,256,4]{1,2,0:T(4,128)S(1)}, ...) while((s32[]{:T(128)}, f32[256,4]{0,1:T(4,128)S(1)}, ...), condition=%wide.region_26.27_spmd, body=%wide.region_25.26_spmd.sunk | while | flops 399365 | bytes 2678935 | solution.py:24
  799.0 65.0 %all-reduce.11.cloned.1.call-done = f32[256,128]{1,0:T(8,128)} async-done(((f32[256,128]{1,0:T(8,128)}), f32[256,128]{1,0:T(8,128)}) %all-reduce.11.cloned.1.call-update) | async-done | bytes 131088 | tf_op jit(solution)/shard_map/psum | solution.py:199
  864.0 1.5 fusion.63
  (423 shorter events, 199.2 us)
Async XLA Ops:
  7.2 185.7 %all-reduce.5.cloned.1.call-start = ((), (), s32[]{:S(2)}) async-start(), calls=%async_computation | async-start | bytes 1572864 | tf_op jit(solution)/shard_map/psum | solution.py:111
  78.1 209.0 %all-gather.3.cloned.1.call-start = ((), (), s32[]{:S(2)}) async-start(), calls=%async_computation.1 | async-start | bytes 17301504 | tf_op jit(solution)/shard_map/all_gather | solution.py:18
  194.5 4.4 copy-start.1
  209.3 230.4 %all-reduce.7.cloned.1.call-start = ((), (), s32[]{:S(2)}) async-start(), calls=%async_computation.2 | async-start | bytes 262144 | tf_op jit(solution)/shard_map/psum | solution.py:199
  288.5 84.1 %copy-start.2 = (bf16[2,512,128]{2,1,0:T(8,128)(2,1)S(1)}, bf16[2,512,128]{2,1,0:T(8,128)(2,1)}, u32[]{:S(2)}) copy-start(bf16[2,512,128]{2,1,0:T(8,128)(2,1)} %param.24) | copy-start | bytes 786436
  288.5 151.2 %copy-start = (bf16[256,128]{1,0:T(8,128)(2,1)S(1)}, bf16[256,128]{1,0:T(8,128)(2,1)}, u32[]{:S(2)}) copy-start(bf16[256,128]{1,0:T(8,128)(2,1)} %param.17) | copy-start | bytes 196612
  373.5 243.7 %all-reduce.9.cloned.1.call-start = ((), (), s32[]{:S(2)}) async-start(), calls=%async_computation.3 | async-start | bytes 1572864 | tf_op jit(solution)/shard_map/psum | solution.py:111
  509.7 201.7 %all-gather.5.cloned.1.call-start = ((), (), s32[]{:S(2)}) async-start(), calls=%async_computation.4 | async-start | bytes 17301504 | tf_op jit(solution)/shard_map/all_gather | solution.py:18
  633.6 230.4 %all-reduce.11.cloned.1.call-start = ((), (), s32[]{:S(2)}) async-start(), calls=%async_computation.5 | async-start | bytes 262144 | tf_op jit(solution)/shard_map/psum | solution.py:199
Sparse Core Ops, SparseCore 0:
  78.2 114.5 all-reduce.4
  209.4 77.6 all-gather.2
  373.6 66.0 all-reduce.6
  509.8 107.3 all-reduce.8
  633.7 77.6 all-gather.4
  797.9 66.0 all-reduce.10
where the time goes:
time: 880 us; the launch traced here: 872 us
  waiting for transfers between devices  409 us (46%)
  blocking collectives  228 us (26%)
  other arithmetic  108 us (12%)
  local copies, waits for them, and re-layouts  96.4 us (11%)
  between operations  14.5 us (2%)
  matrix products  13.8 us (2%)
    psum x2, waiting for transfers between devices, on_device(): lax.psum(jnp.dot(normed, w_joined, preferred_element_type=jnp.float32), '...  217 us
    psum x2, blocking collectives, on_device(): square_sum = lax.psum(jnp.sum(wide * wide, axis=1), 'req')  133 us
    psum x2, waiting for transfers between devices, on_device(): branch = lax.psum(partial_out, 'kv')  131 us
    all_gather x4, blocking collectives, joined(): everything = jax.tree.map(lambda part: lax.all_gather(part, axis), array)  95 us
    add x62, other arithmetic, join_partials(): first_num * first_scale[:, :, None] + other_num * other_scale[:, :, None]  78.6 us
    dynamic_slice x62, local copies, waits for them, and re-layouts, step(): return combine(so_far, jax.tree.map(lambda part: part[k], everything))  67.2 us
    all_gather x2, waiting for transfers between devices, joined(): everything = jax.tree.map(lambda part: lax.all_gather(part, axis), array)  60.2 us
  transfers between devices with their start and end apart: 6, of which 6 were waited for; matrix products, arithmetic and copies ran while one was open for 1% of the time, Pallas kernels for 0%

commit v1 on v0

v1 whole, which is shorter than its diff:
```python
import functools
import math

import jax
import jax.numpy as jnp
import numpy as np
from jax import lax
from jax.experimental import pallas as pl
from jax.experimental.pallas import tpu as pltpu
from jax.sharding import PartitionSpec as P

LAYERS = 2
EPS = 1e-06
THETA = 1000000.0
FLOOR = -1e30
CEIL = -1e29
TINY = 1e-30
MESH = pl.DeviceIdType.MESH
F32 = jnp.float32
BF16 = jnp.bfloat16

RS, SQ, QX, PX, HO, LO, LL, ZR, ZA, ZB = range(10)


def dot(a, b):
    return jnp.dot(a, b, preferred_element_type=F32)


def dot_nt(a, b):
    return lax.dot_general(a, b, (((1,), (1,)), ((), ())), preferred_element_type=F32)


def iota(shape, dim):
    return lax.broadcasted_iota(jnp.int32, shape, dim)


def kernel(
    n_chip,
    side,
    nz,
    width,
    x_in, norm_gain, q_gain, k_gain, w_query, w_key, w_value, w_out,
    cache_keys, cache_values, lengths, block_owner, block_fill, frequency,
    out, out_keys, out_values,
    x_own, x_sib, gains, q_gains, k_gains, wq, wk, wv, wo, keys, values,
    lens, owner, fill, freq,
    x_half, long_bias, home_bias, turn_cos, turn_sin, pick, spread,
    rs_s, rs_r, sq_s, sq_r, qx_s, qx_r, px_s, px_r,
    ho_s, ho_r, lo_s, lo_r, ll_s, ll_r, zr_s, zr_r, za_s, fin_s, fin_r,
    load_sem, init_send, init_recv, send_sem, recv_sem,
):
    half = 8 * n_chip
    part = half // nz
    blocks = cache_keys.shape[1]
    total = lens.shape[1]
    me = lax.axis_index("req")
    my_z = lax.axis_index("kv")
    core = me % 2
    chip = me // 2
    chip_x, chip_y = chip // side, chip % side
    sib = me + 1 - 2 * core

    def peer(t):
        px = (chip_x + t // side) % side
        py = (chip_y + t % side) % side
        return (px * side + py) * 2 + core

    def chip_of(t):
        px = (chip_x + t // side) % side
        py = (chip_y + t % side) % side
        return px * side + py

    barrier = pltpu.get_barrier_semaphore()

    def greet(req, kv):
        pl.semaphore_signal(
            barrier, inc=1, device_id={"req": req, "kv": kv}, device_id_type=MESH
        )

    def greet_chip(t, carry):
        greet(peer(t), my_z)
        return carry

    def greet_z(t, carry):
        greet(me, (my_z + t) % nz)
        greet(sib, (my_z + t) % nz)
        return carry

    lax.fori_loop(1, n_chip, greet_chip, 0)
    lax.fori_loop(1, nz, greet_z, 0)
    greet(sib, my_z)

    loads = [
        pltpu.make_async_copy(src, dst, load_sem.at[at])
        for at, (src, dst) in enumerate(
            [
                (lengths, lens),
                (frequency, freq),
                (norm_gain, gains.at[:, pl.ds(0, 128)]),
                (q_gain, q_gains),
                (k_gain, k_gains),
                (x_in, x_own),
                (w_query, wq.at[:, pl.ds(0, 128)]),
                (w_key, wk.at[:, pl.ds(0, 128)]),
                (w_value, wv.at[:, pl.ds(0, 128)]),
                (block_owner, owner),
                (block_fill, fill),
                (cache_keys.at[0], keys.at[0, pl.ds(0, blocks)]),
                (cache_values.at[0], values.at[0, pl.ds(0, blocks)]),
                (w_out, wo.at[:, 0]),
                (cache_keys.at[1], keys.at[1, pl.ds(0, blocks)]),
                (cache_values.at[1], values.at[1, pl.ds(0, blocks)]),
            ]
        )
    ]
    for copy in loads:
        copy.start()

    loads[0].wait()
    loads[1].wait()
    length_row = lens[...].astype(F32)
    request_row = iota((8, total), 1).astype(F32)
    is_long = jnp.where(length_row > 128.0, 1.0, 0.0)
    before = jnp.where(iota((total, total), 0) < iota((total, total), 1), 1.0, 0.0).astype(BF16)
    rank = dot(jnp.broadcast_to(is_long, (8, total)).astype(BF16), before)
    slot8 = iota((8, total), 0)
    long_hot = jnp.where(
        (rank.astype(jnp.int32) == slot8) & (slot8 < 4),
        jnp.broadcast_to(is_long, (8, total)),
        0.0,
    )
    own_hot = jnp.where(iota((8, total), 1) == 8 * me + slot8, 1.0, 0.0)
    long_id = jnp.sum(long_hot * request_row, axis=1, keepdims=True)
    long_at = jnp.sum(long_hot * length_row, axis=1, keepdims=True)
    own_at = jnp.sum(own_hot * length_row, axis=1, keepdims=True)
    own_keep = jnp.where(own_at > 128.0, 0.0, 1.0)
    row_of = iota((total, 128), 1)
    to_half = jnp.where(
        (iota((total, 128), 0) == (row_of // 8) * 16 + 8 * core + row_of % 8) & (row_of < half),
        1.0,
        0.0,
    ).astype(BF16)
    long_half = dot(long_hot.astype(BF16), to_half)
    own_half = jnp.where(iota((8, 128), 1) == 8 * chip + iota((8, 128), 0), 1.0, 0.0)
    pick[...] = jnp.concatenate([own_half, long_half], axis=0)
    four = jnp.where(iota((8, 128), 0) < 4, long_half, pltpu.roll(long_half, 4, 0))
    eye = jnp.where(iota((half, 128), 0) == iota((half, 128), 1), 1.0, 0.0)
    spread[...] = dot_nt(
        eye.astype(BF16), jnp.concatenate([four, four], axis=0).astype(BF16)
    ).astype(BF16)
    long_sel = jnp.concatenate([long_half, jnp.zeros((8, 128), F32)], axis=0).astype(BF16)
    long_sel = long_sel[:, :half]
    angle = jnp.concatenate([own_at, long_at], axis=0) * freq[...]
    turn_cos[...] = jnp.cos(angle)
    turn_sin[...] = jnp.where(iota((16, 128), 1) < 64, -jnp.sin(angle), jnp.sin(angle))

    def half_of(ref):
        rows = ref[...].astype(F32).reshape(n_chip, 2, 8, 128)
        return jnp.where(core == 0, rows[:, 0], rows[:, 1]).reshape(half, 128)

    loads[5].wait()
    x_first = half_of(x_own)

    pl.semaphore_wait(barrier, n_chip - 1 + 2 * (nz - 1) + 1)

    def remote(src, dst, send, recv, req, kv):
        return pltpu.make_async_remote_copy(
            src_ref=src,
            dst_ref=dst,
            send_sem=send,
            recv_sem=recv,
            device_id={"req": req, "kv": kv},
            device_id_type=MESH,
        )

    shares = [
        remote(src, dst, init_send.at[at], init_recv.at[at], sib, my_z)
        for at, (src, dst) in enumerate(
            [
                (x_in, x_sib),
                (norm_gain, gains.at[:, pl.ds(128, 128)]),
                (w_query.at[0], wq.at[0, pl.ds(128, 128)]),
                (w_key.at[0], wk.at[0, pl.ds(128, 128)]),
                (w_value.at[0], wv.at[0, pl.ds(128, 128)]),
                (w_out.at[0], wo.at[0, 1]),
                (w_query.at[1], wq.at[1, pl.ds(128, 128)]),
                (w_key.at[1], wk.at[1, pl.ds(128, 128)]),
                (w_value.at[1], wv.at[1, pl.ds(128, 128)]),
                (w_out.at[1], wo.at[1, 1]),
            ]
        )
    ]
    for copy in shares:
        copy.start()

    for at in (2, 3, 4, 6, 7, 8):
        loads[at].wait()
    shares[0].wait_recv()
    shares[1].wait_recv()
    x_half[0] = (
        jnp.concatenate([x_first, half_of(x_sib)], axis=1).astype(BF16).reshape(nz, part, 256)
    )
    for at in (2, 3, 4):
        shares[at].wait_recv()

    def normed_turned(t, scale, gain, cos, sin):
        t = t * scale
        t = t * lax.rsqrt(jnp.mean(t * t, axis=1, keepdims=True) + EPS) * gain
        return t * cos + pltpu.roll(t, 64, 1) * sin

    def arrived(ref, sem):
        pltpu.make_async_copy(ref, ref, sem).wait()

    def to_chips(pairs, layer):
        def step(t, carry):
            req = peer(t)
            for src, dst, phase in pairs(chip_of(t)):
                remote(
                    src, dst, send_sem.at[layer, phase], recv_sem.at[layer, phase], req, my_z
                ).start()
            return carry

        lax.fori_loop(1, n_chip, step, 0)

    logit = 1.0 / math.sqrt(128)
    others = pl.ds(0, n_chip - 1)
    row16 = iota((16, 128), 0)
    lane16 = iota((16, 128), 1)
    sub8 = iota((8, 128), 0)

    for layer in range(LAYERS):
        x = x_half[layer].reshape(half, 256).astype(F32)
        square = jnp.sum(x * x, axis=1, keepdims=True)
        square_row = jnp.sum(jnp.where(eye > 0.0, square, 0.0), axis=0, keepdims=True)
        sq_s[layer] = square_row
        sq_r[layer, chip] = square_row
        xg = (x * gains[pl.ds(layer, 1), :].astype(F32)).astype(BF16)
        xl = dot(long_sel, xg).astype(BF16)
        if layer == 1:
            for at in (6, 7, 8):
                shares[at].wait_recv()
        q = dot(xg, wq[layer])
        q_long = dot(xl, wq[layer])[0:8]
        kv = jnp.concatenate([dot(xg, wk[layer]), dot(xg, wv[layer])], axis=1)
        low = jnp.concatenate([pltpu.roll(kv, 4, 0), kv], axis=1).reshape(n_chip, 8, 512)
        low = jnp.where(
            iota((n_chip, 8, 512), 1) < 4,
            jnp.broadcast_to(q_long[None], (n_chip, 8, 512)),
            low,
        )
        message = jnp.concatenate([q.reshape(n_chip, 8, 512), low], axis=1).astype(BF16)
        rs_s[layer] = message
        to_chips(
            lambda to: [
                (rs_s.at[layer, to], rs_r.at[layer, chip], RS),
                (sq_s.at[layer], sq_r.at[layer, chip], SQ),
            ],
            layer,
        )
        rs_r[layer, chip] = rs_s[layer, chip]

        if layer == 0:
            loads[9].wait()
            loads[10].wait()
            lane8 = iota((8, 128), 1)

            def block_masks(b, carry):
                live = (lane8 < fill[b]) & (long_id == owner[b].astype(F32)) & (sub8 < 4)
                bias = jnp.where(live, 0.0, FLOOR)
                long_bias[:, pl.ds(pl.multiple_of(b * 128, 128), 128)] = jnp.where(
                    sub8 < 4, bias, pltpu.roll(bias, 4, 0)
                )
                return carry

            lax.fori_loop(0, blocks, block_masks, 0)
            live = (long_id == (8 * me + lane8).astype(F32)) & (lane8 < 8) & (sub8 < 4)
            bias = jnp.where(live, 0.0, FLOOR)
            long_bias[:, pl.ds(blocks * 128, 128)] = jnp.where(
                sub8 < 4, bias, pltpu.roll(bias, 4, 0)
            )
            for b in range(8):
                home_bias[:, pl.ds(b * 128, 128)] = jnp.where(
                    (sub8 == b) & (lane8 < fill[b]), 0.0, FLOOR
                )
            home_bias[:, pl.ds(1024, 128)] = jnp.where(sub8 == lane8, 0.0, FLOOR)
            zero = jnp.zeros((LAYERS, 128, 128), BF16)
            keys[:, blocks] = zero
            values[:, blocks] = zero
            loads[11].wait()
            loads[12].wait()
        else:
            loads[14].wait()
            loads[15].wait()

        arrived(sq_r.at[layer, others], recv_sem.at[layer, SQ])
        arrived(rs_r.at[layer, others], recv_sem.at[layer, RS])
        square_all = jnp.sum(sq_r[layer], axis=0)
        scale = lax.rsqrt(
            jnp.sum(pick[...] * square_all, axis=1, keepdims=True) / width + EPS
        )
        sums = jnp.sum(rs_r[layer].astype(F32), axis=0)
        q_gain_row = q_gains[pl.ds(layer, 1), :].astype(F32)
        turned = [
            normed_turned(
                sums[:, 128 * g : 128 * g + 128], scale, q_gain_row, turn_cos[...], turn_sin[...]
            )
            for g in range(4)
        ]
        q_far = [t[8:16] for t in turned]
        q_far = jnp.concatenate(
            [
                jnp.where(sub8 < 4, q_far[0], pltpu.roll(q_far[1], 4, 0)),
                jnp.where(sub8 < 4, q_far[2], pltpu.roll(q_far[3], 4, 0)),
            ],
            axis=0,
        ).astype(BF16)
        qx_s[layer] = q_far
        q_share = remote(
            qx_s.at[layer], qx_r.at[layer], send_sem.at[layer, QX], recv_sem.at[layer, QX],
            sib, my_z,
        )
        q_share.start()

        q_own = jnp.concatenate([t[0:8] for t in turned], axis=0).astype(BF16)
        low = sums[8:16]
        kv = jnp.where(iota((8, 256), 0) < 4, pltpu.roll(low[:, 0:256], 4, 0), low[:, 256:512])
        new_key = normed_turned(
            kv[:, 0:128],
            scale[0:8],
            k_gains[pl.ds(layer, 1), :].astype(F32),
            turn_cos[0:8, :],
            turn_sin[0:8, :],
        )
        new_value = kv[:, 128:256] * scale[0:8]
        out_keys[layer] = new_key.astype(BF16)
        out_values[layer] = new_value.astype(BF16)
        pad = jnp.zeros((8, 128), F32)
        keys[layer, blocks, 0:16] = jnp.concatenate([new_key, pad], axis=0).astype(BF16)
        values[layer, blocks, 0:16] = jnp.concatenate([new_value, pad], axis=0).astype(BF16)

        s = jnp.concatenate(
            [
                dot_nt(q_own, keys[layer, 0:8].reshape(1024, 128)),
                dot_nt(q_own, keys[layer, blocks]),
            ],
            axis=1,
        )
        s = s * logit + jnp.concatenate([home_bias[...]] * 4, axis=0)
        p = jnp.exp(s - jnp.max(s, axis=1, keepdims=True))
        den = jnp.sum(p, axis=1, keepdims=True)
        p = p.astype(BF16)
        num = dot(p[:, 0:1024], values[layer, 0:8].reshape(1024, 128)) + dot(
            p[:, 1024:1152], values[layer, blocks]
        )
        attended = (num * (jnp.concatenate([own_keep] * 4, axis=0) / den)).astype(BF16)
        ho_s[layer] = attended
        ho_r[layer, chip] = attended
        to_chips(lambda to: [(ho_s.at[layer], ho_r.at[layer, chip], HO)], layer)

        q_share.wait_recv()
        q_all = q_far + qx_r[layer]
        s = dot_nt(q_all, keys[layer].reshape((blocks + 1) * 128, 128))
        s = s * logit + jnp.concatenate([long_bias[...]] * 2, axis=0)
        top = jnp.maximum(jnp.max(s, axis=1, keepdims=True), CEIL)
        p = jnp.exp(s - top)
        den = jnp.sum(p, axis=1, keepdims=True)
        num = dot(p.astype(BF16), values[layer].reshape((blocks + 1) * 128, 128))
        level = jnp.where(den > 0.0, top + jnp.log(jnp.maximum(den, TINY)), FLOOR)
        level = jnp.broadcast_to(level, (16, 128))
        mean = num / jnp.maximum(den, TINY)
        px_s[layer] = jnp.concatenate([mean, level], axis=0)
        p_share = remote(
            px_s.at[layer], px_r.at[layer], send_sem.at[layer, PX], recv_sem.at[layer, PX],
            sib, my_z,
        )
        p_share.start()
        p_share.wait_recv()
        other_mean, other_level = px_r[layer, 0:16], px_r[layer, 16:32]
        top = jnp.maximum(level, other_level)
        mine, theirs = jnp.exp(level - top), jnp.exp(other_level - top)
        both = mine + theirs
        mean = ((mean * mine + other_mean * theirs) / both).astype(BF16)
        level = top + jnp.log(both)
        level_row = jnp.sum(jnp.where(row16 == lane16, level, 0.0), axis=0, keepdims=True)
        lo_s[layer] = mean
        lo_r[layer, chip] = mean
        ll_s[layer] = level_row
        ll_r[layer, chip] = level_row
        to_chips(
            lambda to: [
                (lo_s.at[layer], lo_r.at[layer, chip], LO),
                (ll_s.at[layer], ll_r.at[layer, chip], LL),
            ],
            layer,
        )

        if layer == 0:
            loads[13].wait()
        shares[5 if layer == 0 else 9].wait_recv()
        arrived(ho_r.at[layer, others], recv_sem.at[layer, HO])
        homes = ho_r[layer].astype(F32)
        homes = jnp.concatenate(
            [homes[:, 8 * g : 8 * g + 8].reshape(half, 128) for g in range(4)], axis=1
        )
        arrived(ll_r.at[layer, others], recv_sem.at[layer, LL])
        arrived(lo_r.at[layer, others], recv_sem.at[layer, LO])
        levels = ll_r[layer]
        weight = jnp.exp(levels - jnp.max(levels, axis=0, keepdims=True))
        weight = weight / jnp.sum(weight, axis=0, keepdims=True)
        weight = jnp.sum(
            jnp.where(
                iota((n_chip, 16, 128), 1) == iota((n_chip, 16, 128), 2),
                jnp.broadcast_to(weight, (n_chip, 16, 128)),
                0.0,
            ),
            axis=2,
            keepdims=True,
        )
        merged = jnp.sum(weight * lo_r[layer].astype(F32), axis=0)
        merged = jnp.concatenate(
            [jnp.where(row16 // 4 == g, merged, 0.0) for g in range(4)], axis=1
        ).astype(BF16)
        attended = (homes + dot(spread[...], merged)).astype(BF16)

        branch = jnp.concatenate(
            [dot(attended, wo[layer, 0]), dot(attended, wo[layer, 1])], axis=1
        )
        zr_s[layer] = branch.astype(BF16).reshape(nz, part, 256)

        def reduce_z(t, carry):
            to = (my_z + t) % nz
            remote(
                zr_s.at[layer, to], zr_r.at[layer, my_z],
                send_sem.at[layer, ZR], recv_sem.at[layer, ZR], me, to,
            ).start()
            return carry

        lax.fori_loop(1, nz, reduce_z, 0)
        zr_r[layer, my_z] = zr_s[layer, my_z]
        arrived(zr_r.at[layer, pl.ds(0, nz - 1)], recv_sem.at[layer, ZR])
        hidden = (
            x_half[layer, my_z].astype(F32) + jnp.sum(zr_r[layer].astype(F32), axis=0)
        ).astype(BF16)

        if layer + 1 < LAYERS:
            za_s[...] = hidden
            x_half[layer + 1, my_z] = hidden

            def gather_z(t, carry):
                to = (my_z + t) % nz
                remote(
                    za_s, x_half.at[layer + 1, my_z],
                    send_sem.at[layer, ZA], recv_sem.at[layer, ZA], me, to,
                ).start()
                return carry

            lax.fori_loop(1, nz, gather_z, 0)
            arrived(x_half.at[layer + 1, pl.ds(0, nz - 1)], recv_sem.at[layer, ZA])
        else:
            mine, theirs = hidden[:, 0:128], hidden[:, 128:256]
            fin_s[0] = mine
            fin_s[1] = theirs
            fin_r[0, my_z] = mine

            def finish_z(t, carry):
                to = (my_z + t) % nz
                remote(
                    fin_s.at[1], fin_r.at[1, my_z],
                    send_sem.at[layer, ZB], recv_sem.at[layer, ZB], sib, to,
                ).start()
                remote(
                    fin_s.at[0], fin_r.at[0, my_z],
                    send_sem.at[layer, ZA], recv_sem.at[layer, ZA], me, to,
                ).start()
                return carry

            lax.fori_loop(1, nz, finish_z, 0)
            remote(
                fin_s.at[1], fin_r.at[1, my_z],
                send_sem.at[layer, ZB], recv_sem.at[layer, ZB], sib, my_z,
            ).start()
            arrived(fin_r.at[0, pl.ds(0, nz - 1)], recv_sem.at[layer, ZA])
            arrived(fin_r.at[1], recv_sem.at[layer, ZB])
            near = fin_r[0].astype(F32).reshape(n_chip, 8, 128)
            far = fin_r[1].astype(F32).reshape(n_chip, 8, 128)
            out[...] = (
                jnp.concatenate(
                    [jnp.where(core == 0, near, far), jnp.where(core == 0, far, near)], axis=1
                )
                .reshape(total, 128)
                .astype(BF16)
            )

    for copy in shares:
        copy.wait_send()
    for layer in range(LAYERS):
        for ref, phase in (
            (rs_r.at[layer, others], RS),
            (sq_r.at[layer, others], SQ),
            (qx_r.at[layer], QX),
            (px_r.at[layer], PX),
            (ho_r.at[layer, others], HO),
            (lo_r.at[layer, others], LO),
            (ll_r.at[layer, others], LL),
            (zr_r.at[layer, pl.ds(0, nz - 1)], ZR),
        ):
            arrived(ref, send_sem.at[layer, phase])
        if layer + 1 < LAYERS:
            arrived(x_half.at[layer + 1, pl.ds(0, nz - 1)], send_sem.at[layer, ZA])
        else:
            arrived(fin_r.at[0, pl.ds(0, nz - 1)], send_sem.at[layer, ZA])
            arrived(fin_r.at[1], send_sem.at[layer, ZB])


def on_device(
    n_chip, side, nz, width,
    hidden_in, norm_gain, q_gain, k_gain, w_query, w_key, w_value, w_out,
    cache_keys, cache_values, lengths, block_owner, block_fill,
):
    half = 8 * n_chip
    part = half // nz
    blocks = cache_keys.shape[1]
    total = hidden_in.shape[0]
    heads = w_query.shape[2]
    exponent = np.concatenate([np.arange(64), np.arange(64)]) * 2.0 / 128
    frequency = jnp.asarray((THETA**-exponent).astype(np.float32)[None, :])
    vmem, sem = pltpu.VMEM, pltpu.SemaphoreType.DMA
    anywhere = pl.BlockSpec(memory_space=pl.ANY)
    onchip = pl.BlockSpec(memory_space=pltpu.VMEM)
    both = (LAYERS, n_chip)
    return pl.pallas_call(
        functools.partial(kernel, n_chip, side, nz, float(width)),
        out_shape=(
            jax.ShapeDtypeStruct((total, 128), BF16),
            jax.ShapeDtypeStruct((LAYERS, 8, 128), BF16),
            jax.ShapeDtypeStruct((LAYERS, 8, 128), BF16),
        ),
        in_specs=[anywhere] * 14,
        out_specs=(onchip, onchip, onchip),
        scratch_shapes=[
            vmem((total, 128), BF16),
            vmem((total, 128), BF16),
            vmem((LAYERS, 256), BF16),
            vmem((LAYERS, 128), BF16),
            vmem((LAYERS, 128), BF16),
            vmem((LAYERS, 256, heads), BF16),
            vmem((LAYERS, 256, 128), BF16),
            vmem((LAYERS, 256, 128), BF16),
            vmem((LAYERS, 2, heads, 128), BF16),
            vmem((LAYERS, blocks + 1, 128, 128), BF16),
            vmem((LAYERS, blocks + 1, 128, 128), BF16),
            vmem((1, total), jnp.int32),
            pltpu.SMEM((blocks,), jnp.int32),
            pltpu.SMEM((blocks,), jnp.int32),
            vmem((1, 128), F32),
            vmem((LAYERS, nz, part, 256), BF16),
            vmem((8, (blocks + 1) * 128), F32),
            vmem((8, 9 * 128), F32),
            vmem((16, 128), F32),
            vmem((16, 128), F32),
            vmem((16, 128), F32),
            vmem((half, 16), BF16),
            vmem((*both, 16, 512), BF16),
            vmem((*both, 16, 512), BF16),
            vmem((LAYERS, 1, 128), F32),
            vmem((*both, 1, 128), F32),
            vmem((LAYERS, 16, 128), BF16),
            vmem((LAYERS, 16, 128), BF16),
            vmem((LAYERS, 32, 128), F32),
            vmem((LAYERS, 32, 128), F32),
            vmem((LAYERS, 32, 128), BF16),
            vmem((*both, 32, 128), BF16),
            vmem((LAYERS, 16, 128), BF16),
            vmem((*both, 16, 128), BF16),
            vmem((LAYERS, 1, 128), F32),
            vmem((*both, 1, 128), F32),
            vmem((LAYERS, nz, part, 256), BF16),
            vmem((LAYERS, nz, part, 256), BF16),
            vmem((part, 256), BF16),
            vmem((2, part, 128), BF16),
            vmem((2, nz, part, 128), BF16),
            sem((16,)),
            sem((10,)),
            sem((10,)),
            sem((LAYERS, 10)),
            sem((LAYERS, 10)),
        ],
        compiler_params=pltpu.CompilerParams(
            collective_id=0, has_side_effects=True, vmem_limit_bytes=48 * 1024 * 1024
        ),
        name="attention_layers",
    )(
        hidden_in, norm_gain, q_gain, k_gain, w_query, w_key, w_value, w_out,
        cache_keys, cache_values, lengths.reshape(1, total), block_owner, block_fill, frequency,
    )


def solution(mesh):
    n_req, nz = mesh.shape["req"], mesh.shape["kv"]
    n_chip = n_req // 2
    side = math.isqrt(n_chip)
    in_specs = (
        P(None, "req"),
        P(None, "req"),
        P(),
        P(),
        P(None, "req", "kv"),
        P(None, "req", "kv"),
        P(None, "req", "kv"),
        P(None, "kv", "req"),
        P(None, "req", None, "kv"),
        P(None, "req", None, "kv"),
        P(),
        P("req"),
        P("req"),
    )
    out_specs = (P(None, "req"), P(None, "req", "kv"), P(None, "req", "kv"))
    return jax.shard_map(
        functools.partial(on_device, n_chip, side, nz, 128 * n_req),
        mesh=mesh,
        in_specs=in_specs,
        out_specs=out_specs,
        check_vma=False,
    )
```

time: 880 us -> 77 us (0.09)
  waiting for transfers between devices: 409 us -> 0 us
  blocking collectives: 228 us -> 0 us
  other arithmetic: 108 us -> 0 us
  local copies, waits for them, and re-layouts: 96.4 us -> 12.7 us
  Pallas kernels: 0 us -> 63.2 us
  between operations: 14.5 us -> 0.67 us
  matrix products: 13.8 us -> 0 us
    psum x4 -> x0, waiting for transfers between devices: 348 us -> none  [the longest x2 217 us: on_device(): lax.psum(jnp.dot(normed, w_joined, preferred_element_type=jnp.float32), '...]
    psum x2 -> x0, blocking collectives: 133 us -> none  [on_device(): square_sum = lax.psum(jnp.sum(wide * wide, axis=1), 'req')]
    all_gather x4 -> x0, blocking collectives: 95 us -> none  [joined(): everything = jax.tree.map(lambda part: lax.all_gather(part, axis), array)]
    add x124 -> x0, other arithmetic: 80.3 us -> none  [the longest x62 78.6 us: join_partials(): first_num * first_scale[:, :, None] + other_num * other_scale[:, :, None]]
    dynamic_slice x62 -> x0, local copies, waits for them, and re-layouts: 67.2 us -> none  [step(): return combine(so_far, jax.tree.map(lambda part: part[k], everything))]
    pallas_call x0 -> x1, Pallas kernels: none -> 63.2 us  [on_device(): pl.pallas_call(functools.partial(kernel, n_chip, side, nz, float(width)),...]
    all_gather x2 -> x0, waiting for transfers between devices: 60.2 us -> none  [joined(): everything = jax.tree.map(lambda part: lax.all_gather(part, axis), array)]
    exp x124 -> x0, local copies, waits for them, and re-layouts: 16.8 us -> none  [the longest x62 8.58 us: join_partials(): first_scale = jnp.exp(first_max - joint_max)]
  transfers between devices with their start and end apart: 6 -> 0, of which waited for: 6 -> 0; matrix products, arithmetic and copies ran while one was open for 1% -> 0% of each run, Pallas kernels for 0% -> 0%
where the time goes in v1:
time: 77 us; the launch traced here: 76.6 us
  Pallas kernels  63.2 us (82%)
  local copies, waits for them, and re-layouts  12.7 us (16%)
    pallas_call x1, Pallas kernels, on_device(): pl.pallas_call(functools.partial(kernel, n_chip, side, nz, float(width)),...  63.2 us
    unnamed x29, local copies, waits for them, and re-layouts  12.7 us

profile of v1, /device:TPU:1, one launch (start us, length us, event | category | flops | bytes accessed | tf_op | source)
XLA Modules:
  0.0 76.6 jit_solution(9140122606618156110)
XLA Ops:
  0.6 0.0 copy-start
  0.6 1.9 %copy-done = bf16[2,48,128,128]{3,2,1,0:T(8,128)(2,1)S(1)} copy-done((bf16[2,48,128,128]{3,2,1,0:T(8,128)(2,1)S(1)}, bf16[2,48,128,128]{3,2,1,0:T(8,128)(2,1)}, u32[]{:S(2)}) %copy-start) | copy-done | bytes 3145752
  2.5 0.0 copy-start.1
  2.5 0.9 %copy-done.1 = bf16[2,128,512]{2,1,0:T(8,128)(2,1)S(1)} copy-done((bf16[2,128,512]{2,1,0:T(8,128)(2,1)S(1)}, bf16[2,128,512]{2,1,0:T(8,128)(2,1)}, u32[]{:S(2)}) %copy-start.1) | copy-done | bytes 262168
  3.5 0.0 copy-start.2
  3.5 0.9 %copy-done.2 = bf16[2,512,128]{2,1,0:T(8,128)(2,1)S(1)} copy-done((bf16[2,512,128]{2,1,0:T(8,128)(2,1)S(1)}, bf16[2,512,128]{2,1,0:T(8,128)(2,1)}, u32[]{:S(2)}) %copy-start.2) | copy-done | bytes 262168
  4.4 0.0 copy-start.3
  4.4 0.8 %copy-done.3 = bf16[256,128]{1,0:T(8,128)(2,1)S(1)} copy-done((bf16[256,128]{1,0:T(8,128)(2,1)S(1)}, bf16[256,128]{1,0:T(8,128)(2,1)}, u32[]{:S(2)}) %copy-start.3) | copy-done | bytes 65560
  5.3 0.0 copy-start.4
  5.3 0.8 %copy-done.4 = bf16[2,128,128]{2,1,0:T(8,128)(2,1)S(1)} copy-done((bf16[2,128,128]{2,1,0:T(8,128)(2,1)S(1)}, bf16[2,128,128]{2,1,0:T(8,128)(2,1)}, u32[]{:S(2)}) %copy-start.4) | copy-done | bytes 65560
  6.1 0.0 copy-start.5
  6.1 0.8 %copy-done.5 = bf16[2,128,128]{2,1,0:T(8,128)(2,1)S(1)} copy-done((bf16[2,128,128]{2,1,0:T(8,128)(2,1)S(1)}, bf16[2,128,128]{2,1,0:T(8,128)(2,1)}, u32[]{:S(2)}) %copy-start.5) | copy-done | bytes 65560
  6.9 0.0 copy-start.6
  6.9 0.7 copy-done.6
  7.6 0.7 copy-done.7
  8.3 0.7 copy-done.8
  8.9 0.7 copy-done.9
  9.6 0.7 copy-done.10
  10.3 0.7 copy-done.11
  10.9 0.7 copy-done.12
  11.6 63.2 %attention_layers.1 = (bf16[256,128]{1,0:T(8,128)(2,1)S(1)}, bf16[2,8,128]{2,1,0:T(8,128)(2,1)S(1)}, bf16[2,8,128]{2,1,0:T(8,128)(2,1)S(1)}) custom-call(bf16[256,128]{1,0:T(8,128)(2,1)S(1)} %copy-done.3, bf16[2,128]{1,0:T(2,128)(2,1)S(1)} %copy-done.7, bf16[2,128]{1,0:T(2,128)(2,1)S(1)} %copy-done.8, bf16[2,128]{1,0:T(2,128)(2,1)S(1)} %copy-done.9, ...), custom_call_target="tpu_custom_call" | custom-call | tf_op jit(solution)/shard_map/attention_layers/pallas_call | solution.py:531
  74.7 0.6 copy.20
  75.4 0.6 copy.21
  76.0 0.6 copy.22
  (6 shorter events, 0.0 us)
Async XLA Ops:
  0.6 1.9 %copy-start = (bf16[2,48,128,128]{3,2,1,0:T(8,128)(2,1)S(1)}, bf16[2,48,128,128]{3,2,1,0:T(8,128)(2,1)}, u32[]{:S(2)}) copy-start(bf16[2,48,128,128]{3,2,1,0:T(8,128)(2,1)} %cache_keys.1) | copy-start | bytes 9437188
  2.5 0.9 %copy-start.1 = (bf16[2,128,512]{2,1,0:T(8,128)(2,1)S(1)}, bf16[2,128,512]{2,1,0:T(8,128)(2,1)}, u32[]{:S(2)}) copy-start(bf16[2,128,512]{2,1,0:T(8,128)(2,1)} %w_query.1) | copy-start | bytes 786436
  3.5 0.9 %copy-start.2 = (bf16[2,512,128]{2,1,0:T(8,128)(2,1)S(1)}, bf16[2,512,128]{2,1,0:T(8,128)(2,1)}, u32[]{:S(2)}) copy-start(bf16[2,512,128]{2,1,0:T(8,128)(2,1)} %w_out.1) | copy-start | bytes 786436
  4.4 0.8 %copy-start.3 = (bf16[256,128]{1,0:T(8,128)(2,1)S(1)}, bf16[256,128]{1,0:T(8,128)(2,1)}, u32[]{:S(2)}) copy-start(bf16[256,128]{1,0:T(8,128)(2,1)} %x_in.1) | copy-start | bytes 196612
  5.3 0.8 %copy-start.4 = (bf16[2,128,128]{2,1,0:T(8,128)(2,1)S(1)}, bf16[2,128,128]{2,1,0:T(8,128)(2,1)}, u32[]{:S(2)}) copy-start(bf16[2,128,128]{2,1,0:T(8,128)(2,1)} %w_key.1) | copy-start | bytes 196612
  6.1 0.8 %copy-start.5 = (bf16[2,128,128]{2,1,0:T(8,128)(2,1)S(1)}, bf16[2,128,128]{2,1,0:T(8,128)(2,1)}, u32[]{:S(2)}) copy-start(bf16[2,128,128]{2,1,0:T(8,128)(2,1)} %w_value.1) | copy-start | bytes 196612
  6.9 0.7 copy-start.6
  7.6 0.7 copy-start.7
  8.3 0.7 copy-start.8
  8.9 0.7 copy-start.9
  9.6 0.7 copy-start.10
  10.2 0.7 copy-start.11
  10.9 0.7 copy-start.12

commit v2 on v1

--- a/solution.py
+++ b/solution.py
@@ -586,7 +586,7 @@
             sem((LAYERS, 10)),
         ],
         compiler_params=pltpu.CompilerParams(
-            collective_id=0, has_side_effects=True, vmem_limit_bytes=48 * 1024 * 1024
+            collective_id=0, has_side_effects=True, vmem_limit_bytes=67043328
         ),
         name="attention_layers",
     )(

time: 77 us -> 69.4 us (0.901)
  local copies, waits for them, and re-layouts: 12.7 us -> 4.02 us
  Pallas kernels: 63.2 us -> 64.5 us
    unnamed x29 -> x3, local copies, waits for them, and re-layouts: 12.7 us -> 4.02 us
    pallas_call x1, Pallas kernels: 63.2 us -> 64.5 us  [on_device(): pl.pallas_call(functools.partial(kernel, n_chip, side, nz, float(width)),...]
where the time goes in v2:
time: 69.4 us; the launch traced here: 69.2 us
  Pallas kernels  64.5 us (93%)
  local copies, waits for them, and re-layouts  4.02 us (6%)
    pallas_call x1, Pallas kernels, on_device(): pl.pallas_call(functools.partial(kernel, n_chip, side, nz, float(width)),...  64.5 us
    unnamed x3, local copies, waits for them, and re-layouts  4.02 us

profile of v2, /device:TPU:1, one launch (start us, length us, event | category | flops | bytes accessed | tf_op | source)
XLA Modules:
  0.0 69.2 jit_solution(110971481722684661)
XLA Ops:
  0.6 64.5 %attention_layers.1 = (bf16[256,128]{1,0:T(8,128)(2,1)}, bf16[2,8,128]{2,1,0:T(8,128)(2,1)}, bf16[2,8,128]{2,1,0:T(8,128)(2,1)}) custom-call(bf16[256,128]{1,0:T(8,128)(2,1)} %x_in.1, bf16[2,128]{1,0:T(2,128)(2,1)} %norm_gain.1, bf16[2,128]{1,0:T(2,128)(2,1)} %q_gain.1, bf16[2,128]{1,0:T(2,128)(2,1)} %k_gain.1, bf16[2,128,512]{2,1,0:T(8,128)(2,1)} %w_query.1, ...), custom_call_target="tpu_custom_call" | custom-call | tf_op jit(solution)/shard_map/attention_layers/pallas_call | solution.py:531
  65.2 1.5 %copy.20 = bf16[256,128]{1,0:T(8,128)(2,1)} copy(bf16[256,128]{1,0:T(8,128)(2,1)} %get-tuple-element.6) | data formatting | bytes 131072
  66.6 1.3 %copy.21 = bf16[2,8,128]{2,1,0:T(8,128)(2,1)} copy(bf16[2,8,128]{2,1,0:T(8,128)(2,1)} %get-tuple-element.7) | data formatting | bytes 8192
  67.9 1.3 %copy.22 = bf16[2,8,128]{2,1,0:T(8,128)(2,1)} copy(bf16[2,8,128]{2,1,0:T(8,128)(2,1)} %get-tuple-element.8) | data formatting | bytes 8192

commit v3 on v2

v3 whole, which is shorter than its diff:
```python
import functools
import math

import jax
import jax.numpy as jnp
import numpy as np
from jax import lax
from jax.experimental import pallas as pl
from jax.experimental.pallas import tpu as pltpu
from jax.sharding import PartitionSpec as P

LAYERS = 2
EPS = 1e-06
THETA = 1000000.0
FLOOR = -1e30
CEIL = -1e29
TINY = 1e-30
MESH = pl.DeviceIdType.MESH
F32 = jnp.float32
BF16 = jnp.bfloat16

RS, SQ, RL, SL, XL, PX, HO, LO, LL, ZR, ZA, ZB = range(12)


def dot(a, b):
    return jnp.dot(a, b, preferred_element_type=F32)


def dot_nt(a, b):
    return lax.dot_general(a, b, (((1,), (1,)), ((), ())), preferred_element_type=F32)


def iota(shape, dim):
    return lax.broadcasted_iota(jnp.int32, shape, dim)


def kernel(
    n_chip,
    side,
    nz,
    width,
    x_in, norm_gain, q_gain, k_gain, w_query, w_key, w_value, w_out,
    cache_keys, cache_values, lengths, block_owner, block_fill, frequency,
    out, out_keys, out_values,
    x_own, x_sib, gains, q_gains, k_gains, wq, wk, wv, wo, keys, values,
    lens, owner, fill, freq,
    x_half, long_bias, home_bias, own_cos, own_sin, long_cos, long_sin, own_pick, spread,
    rs_s, rs_r, sq_s, sq_r, rl_s, rl_r, sl_s, sl_r, xl_s, xl_r, px_s, px_r,
    ho_s, ho_r, lo_s, lo_r, ll_s, ll_r, zr_s, zr_r, za_s, fin_s, new_s,
    load_sem, new_sem, init_send, init_recv, send_sem, recv_sem,
):
    half = 8 * n_chip
    owners = nz // 2
    part = half // owners
    blocks = cache_keys.shape[1]
    total = lens.shape[1]
    me = lax.axis_index("req")
    my_z = lax.axis_index("kv")
    core = lax.rem(me, 2)
    chip = lax.div(me, 2)
    chip_x, chip_y = lax.div(chip, side), lax.rem(chip, side)
    sib = me + 1 - 2 * core
    my_part = lax.rem(my_z, owners)

    def ring(d, n):
        return min(d, n - d)

    steps = sorted(
        [(dx, dy) for dx in range(side) for dy in range(side) if dx or dy],
        key=lambda d: -ring(d[0], side) - ring(d[1], side),
    )
    at_x = [lax.rem(chip_x + d, side) * side for d in range(side)]
    at_y = [lax.rem(chip_y + d, side) for d in range(side)]
    chips = [at_x[dx] + at_y[dy] for dx, dy in steps]
    peers = [2 * c + core for c in chips]
    z_at = [lax.rem(my_z + d, nz) for d in range(nz)]
    z_far = sorted(range(1, nz), key=lambda d: -ring(d, nz))
    z_near = {8: (6, 2, 7, 1), 2: ()}[nz]

    barrier = pltpu.get_barrier_semaphore()

    def greet(req, kv):
        pl.semaphore_signal(
            barrier, inc=1, device_id={"req": req, "kv": kv}, device_id_type=MESH
        )

    for req in peers:
        greet(req, my_z)
    for d in z_far:
        greet(me, z_at[d])
    for d in z_near:
        greet(sib, z_at[d])
    greet(sib, my_z)

    loads = [
        pltpu.make_async_copy(src, dst, load_sem.at[at])
        for at, (src, dst) in enumerate(
            [
                (lengths, lens),
                (frequency, freq),
                (norm_gain, gains.at[:, pl.ds(0, 128)]),
                (q_gain, q_gains),
                (k_gain, k_gains),
                (x_in, x_own),
                (w_query, wq.at[:, pl.ds(0, 128)]),
                (w_key, wk.at[:, pl.ds(0, 128)]),
                (w_value, wv.at[:, pl.ds(0, 128)]),
                (block_owner, owner),
                (block_fill, fill),
                (cache_keys.at[0], keys.at[0, pl.ds(0, blocks)]),
                (cache_values.at[0], values.at[0, pl.ds(0, blocks)]),
                (w_out, wo.at[:, 0]),
                (cache_keys.at[1], keys.at[1, pl.ds(0, blocks)]),
                (cache_values.at[1], values.at[1, pl.ds(0, blocks)]),
            ]
        )
    ]
    for copy in loads:
        copy.start()

    row16 = iota((16, 128), 0)
    lane16 = iota((16, 128), 1)
    sub8 = iota((8, 128), 0)
    lane8 = iota((8, 128), 1)

    def twice(t):
        return jnp.where(iota(t[0].shape, 0) < 4, t[0], pltpu.roll(t[1], 4, 0))

    loads[0].wait()
    loads[1].wait()
    length_row = lens[...].astype(F32)
    request_row = iota((8, total), 1).astype(F32)
    is_long = jnp.where(length_row > 128.0, 1.0, 0.0)
    before = jnp.where(iota((total, total), 0) < iota((total, total), 1), 1.0, 0.0).astype(BF16)
    rank = dot(jnp.broadcast_to(is_long, (8, total)).astype(BF16), before)
    slot8 = iota((8, total), 0)
    long_hot = jnp.where(
        (rank.astype(jnp.int32) == slot8) & (slot8 < 4),
        jnp.broadcast_to(is_long, (8, total)),
        0.0,
    )
    own_hot = jnp.where(iota((8, total), 1) == 8 * me + slot8, 1.0, 0.0)
    long_id = jnp.sum(long_hot * request_row, axis=1, keepdims=True)
    long_at = jnp.sum(long_hot * length_row, axis=1, keepdims=True)
    own_at = jnp.sum(own_hot * length_row, axis=1, keepdims=True)
    own_keep = jnp.where(own_at > 128.0, 0.0, 1.0)
    row_of = iota((total, 128), 1)
    to_half = jnp.where(
        (iota((total, 128), 0) == (row_of // 8) * 16 + 8 * core + row_of % 8) & (row_of < half),
        1.0,
        0.0,
    ).astype(BF16)
    long_half = dot(long_hot.astype(BF16), to_half)
    own_pick[...] = jnp.where(lane8 == 8 * chip + sub8, 1.0, 0.0)
    four = twice([long_half, long_half])
    eye = jnp.where(iota((half, 128), 0) == iota((half, 128), 1), 1.0, 0.0)
    spread[...] = dot_nt(
        eye.astype(BF16), jnp.concatenate([four, four], axis=0).astype(BF16)
    ).astype(BF16)
    long_sel = jnp.concatenate([long_half, jnp.zeros((8, 128), F32)], axis=0).astype(BF16)
    long_sel = long_sel[:, :half]
    long_any = jnp.concatenate([long_hot, jnp.zeros((8, total), F32)], axis=0).astype(BF16)
    long_pick = jnp.where(lane16 == row16 % 4, 1.0, 0.0)

    def turns(at, cos_ref, sin_ref):
        angle = at * freq[...]
        rows = angle.shape[0]
        sin = jnp.sin(angle)
        cos_ref[...] = jnp.cos(angle)
        sin_ref[...] = jnp.where(iota((rows, 128), 1) < 64, -sin, sin)

    turns(own_at, own_cos, own_sin)
    at4 = twice([jnp.broadcast_to(long_at, (8, 128))] * 2)
    turns(jnp.concatenate([at4, at4], axis=0), long_cos, long_sin)

    def half_of(ref):
        rows = ref[...].astype(F32).reshape(n_chip, 2, 8, 128)
        return jnp.where(core == 0, rows[:, 0], rows[:, 1]).reshape(half, 128)

    loads[5].wait()
    x_first = half_of(x_own)
    long_first = dot(long_any, x_own[...])

    pl.semaphore_wait(barrier, len(peers) + len(z_far) + len(z_near) + 1)

    def remote(src, dst, send, recv, req, kv):
        return pltpu.make_async_remote_copy(
            src_ref=src,
            dst_ref=dst,
            send_sem=send,
            recv_sem=recv,
            device_id={"req": req, "kv": kv},
            device_id_type=MESH,
        )

    shares = [
        remote(src, dst, init_send.at[at], init_recv.at[at], sib, my_z)
        for at, (src, dst) in enumerate(
            [
                (x_in, x_sib),
                (norm_gain, gains.at[:, pl.ds(128, 128)]),
                (w_query.at[0], wq.at[0, pl.ds(128, 128)]),
                (w_key.at[0], wk.at[0, pl.ds(128, 128)]),
                (w_value.at[0], wv.at[0, pl.ds(128, 128)]),
                (w_out.at[0], wo.at[0, 1]),
                (w_query.at[1], wq.at[1, pl.ds(128, 128)]),
                (w_key.at[1], wk.at[1, pl.ds(128, 128)]),
                (w_value.at[1], wv.at[1, pl.ds(128, 128)]),
                (w_out.at[1], wo.at[1, 1]),
            ]
        )
    ]
    for copy in shares:
        copy.start()

    for at in (2, 3, 4, 6, 7, 8):
        loads[at].wait()
    shares[0].wait_recv()
    shares[1].wait_recv()
    x_half[0] = (
        jnp.concatenate([x_first, half_of(x_sib)], axis=1).astype(BF16).reshape(owners, part, 256)
    )
    long_x = jnp.concatenate([long_first, dot(long_any, x_sib[...])], axis=1)
    for at in (2, 3, 4):
        shares[at].wait_recv()

    def normed_turned(t, gain, cos, sin):
        t = t * lax.rsqrt(jnp.mean(t * t, axis=1, keepdims=True) + EPS) * gain
        return t * cos + pltpu.roll(t, 64, 1) * sin

    def arrived(ref, sem):
        pltpu.make_async_copy(ref, ref, sem).wait()

    def to_chips(pairs, layer):
        for to, req in zip(chips, peers):
            for src, dst, phase in pairs(to):
                remote(
                    src, dst, send_sem.at[layer, phase], recv_sem.at[layer, phase], req, my_z
                ).start()

    def to_sib(src, dst, phase, layer):
        copy = remote(
            src, dst, send_sem.at[layer, phase], recv_sem.at[layer, phase], sib, my_z
        )
        copy.start()
        return copy

    def as_row(column, mask):
        return jnp.sum(jnp.where(mask, column, 0.0), axis=0, keepdims=True)

    logit = 1.0 / math.sqrt(128)
    others = pl.ds(0, n_chip - 1)
    on_diagonal = iota((half, 128), 0) == iota((half, 128), 1)

    def send_long(layer, long_x):
        square = jnp.sum(long_x * long_x, axis=1, keepdims=True)
        square_row = as_row(square, row16 == lane16)
        sl_s[layer] = square_row
        sl_r[layer, chip] = square_row
        gain = gains[pl.ds(layer, 1), :].astype(F32)
        q = dot((long_x * gain).astype(BF16), wq[layer])[0:8]
        q = [q[:, 128 * g : 128 * g + 128] for g in range(4)]
        q = jnp.concatenate([twice(q[0:2]), twice(q[2:4])], axis=0).astype(BF16)
        rl_s[layer] = q
        rl_r[layer, chip] = q
        to_chips(
            lambda to: [
                (rl_s.at[layer], rl_r.at[layer, chip], RL),
                (sl_s.at[layer], sl_r.at[layer, chip], SL),
            ],
            layer,
        )

    for layer in range(LAYERS):
        x = x_half[layer].reshape(half, 256)
        if layer == 0:
            send_long(layer, long_x)
        else:
            long_x = dot(long_sel, x)
            xl_s[...] = long_x.astype(BF16)
            x_share = to_sib(xl_s, xl_r, XL, layer)
        x = x.astype(F32)
        square = jnp.sum(x * x, axis=1, keepdims=True)
        square_row = as_row(square, on_diagonal)
        sq_s[layer] = square_row
        sq_r[layer, chip] = square_row
        xg = (x * gains[pl.ds(layer, 1), :].astype(F32)).astype(BF16)
        if layer == 1:
            for at in (6, 7, 8):
                shares[at].wait_recv()
        q = dot(xg, wq[layer])
        upper = q[:, 0:384].reshape(n_chip, 8, 384)
        lower = jnp.concatenate(
            [q[:, 384:512], dot(xg, wk[layer]), dot(xg, wv[layer])], axis=1
        ).reshape(n_chip, 8, 384)
        rs_s[layer] = jnp.concatenate([upper, lower], axis=1).astype(BF16)
        to_chips(
            lambda to: [
                (rs_s.at[layer, to], rs_r.at[layer, chip], RS),
                (sq_s.at[layer], sq_r.at[layer, chip], SQ),
            ],
            layer,
        )
        rs_r[layer, chip] = rs_s[layer, chip]

        if layer == 0:
            loads[9].wait()
            loads[10].wait()

            def block_masks(b, carry):
                live = (lane8 < fill[b]) & (long_id == owner[b].astype(F32)) & (sub8 < 4)
                bias = jnp.where(live, 0.0, FLOOR)
                long_bias[:, pl.ds(pl.multiple_of(b * 128, 128), 128)] = twice([bias, bias])
                return carry

            lax.fori_loop(0, blocks, block_masks, 0)
            live = (long_id == (8 * me + lane8).astype(F32)) & (lane8 < 8) & (sub8 < 4)
            bias = jnp.where(live, 0.0, FLOOR)
            long_bias[:, pl.ds(blocks * 128, 128)] = twice([bias, bias])
            for b in range(8):
                home_bias[:, pl.ds(b * 128, 128)] = jnp.where(
                    (sub8 == b) & (lane8 < fill[b]), 0.0, FLOOR
                )
            home_bias[:, pl.ds(1024, 128)] = jnp.where(sub8 == lane8, 0.0, FLOOR)
            zero = jnp.zeros((LAYERS, 128, 128), BF16)
            keys[:, blocks] = zero
            values[:, blocks] = zero
            loads[11].wait()
            loads[12].wait()
        else:
            x_share.wait_recv()
            theirs = xl_r[...].astype(F32)
            send_long(
                layer,
                long_x + jnp.concatenate([theirs[:, 128:256], theirs[:, 0:128]], axis=1),
            )
            loads[14].wait()
            loads[15].wait()

        arrived(sq_r.at[layer, others], recv_sem.at[layer, SQ])
        arrived(rs_r.at[layer, others], recv_sem.at[layer, RS])
        sums = jnp.sum(rs_r[layer].astype(F32), axis=0)
        scale = lax.rsqrt(
            jnp.sum(own_pick[...] * jnp.sum(sq_r[layer], axis=0), axis=1, keepdims=True) / width
            + EPS
        )
        q_gain_row = q_gains[pl.ds(layer, 1), :].astype(F32)
        new_key = normed_turned(
            sums[8:16, 128:256] * scale,
            k_gains[pl.ds(layer, 1), :].astype(F32),
            own_cos[...],
            own_sin[...],
        )
        new_value = sums[8:16, 256:384] * scale
        pad = jnp.zeros((8, 128), F32)
        keys[layer, blocks, 0:16] = jnp.concatenate([new_key, pad], axis=0).astype(BF16)
        values[layer, blocks, 0:16] = jnp.concatenate([new_value, pad], axis=0).astype(BF16)
        new_s[0, layer] = new_key.astype(BF16)
        new_s[1, layer] = new_value.astype(BF16)
        q_own = [
            normed_turned(t * scale, q_gain_row, own_cos[...], own_sin[...])
            for t in (
                sums[0:8, 0:128], sums[0:8, 128:256], sums[0:8, 256:384], sums[8:16, 0:128]
            )
        ]
        q_own = jnp.concatenate(q_own, axis=0).astype(BF16)

        arrived(sl_r.at[layer, others], recv_sem.at[layer, SL])
        arrived(rl_r.at[layer, others], recv_sem.at[layer, RL])
        scale = lax.rsqrt(
            jnp.sum(long_pick * jnp.sum(sl_r[layer], axis=0), axis=1, keepdims=True) / width
            + EPS
        )
        q_long = normed_turned(
            jnp.sum(rl_r[layer].astype(F32), axis=0) * scale,
            q_gain_row,
            long_cos[...],
            long_sin[...],
        ).astype(BF16)
        s = dot_nt(q_long, keys[layer].reshape((blocks + 1) * 128, 128))
        s = s * logit + jnp.concatenate([long_bias[...]] * 2, axis=0)
        top = jnp.maximum(jnp.max(s, axis=1, keepdims=True), CEIL)
        p = jnp.exp(s - top)
        den = jnp.sum(p, axis=1, keepdims=True)
        num = dot(p.astype(BF16), values[layer].reshape((blocks + 1) * 128, 128))
        level = jnp.where(den > 0.0, top + jnp.log(jnp.maximum(den, TINY)), FLOOR)
        level = jnp.broadcast_to(level, (16, 128))
        mean = num / jnp.maximum(den, TINY)
        px_s[layer] = jnp.concatenate([mean, level], axis=0)
        p_share = to_sib(px_s.at[layer], px_r.at[layer], PX, layer)

        s = jnp.concatenate(
            [
                dot_nt(q_own, keys[layer, 0:8].reshape(1024, 128)),
                dot_nt(q_own, keys[layer, blocks]),
            ],
            axis=1,
        )
        s = s * logit + jnp.concatenate([home_bias[...]] * 4, axis=0)
        p = jnp.exp(s - jnp.max(s, axis=1, keepdims=True))
        den = jnp.sum(p, axis=1, keepdims=True)
        p = p.astype(BF16)
        num = dot(p[:, 0:1024], values[layer, 0:8].reshape(1024, 128)) + dot(
            p[:, 1024:1152], values[layer, blocks]
        )
        attended = (num * (jnp.concatenate([own_keep] * 4, axis=0) / den)).astype(BF16)
        ho_s[layer] = attended
        ho_r[layer, chip] = attended
        to_chips(lambda to: [(ho_s.at[layer], ho_r.at[layer, chip], HO)], layer)

        p_share.wait_recv()
        other_mean, other_level = px_r[layer, 0:16], px_r[layer, 16:32]
        top = jnp.maximum(level, other_level)
        mine, theirs = jnp.exp(level - top), jnp.exp(other_level - top)
        both = mine + theirs
        mean = ((mean * mine + other_mean * theirs) / both).astype(BF16)
        level_row = as_row(top + jnp.log(both), row16 == lane16)
        lo_s[layer] = mean
        lo_r[layer, chip] = mean
        ll_s[layer] = level_row
        ll_r[layer, chip] = level_row
        to_chips(
            lambda to: [
                (lo_s.at[layer], lo_r.at[layer, chip], LO),
                (ll_s.at[layer], ll_r.at[layer, chip], LL),
            ],
            layer,
        )

        if layer == 0:
            loads[13].wait()
        else:
            news = [
                pltpu.make_async_copy(new_s.at[at], ref, new_sem.at[at])
                for at, ref in enumerate((out_keys, out_values))
            ]
            for copy in news:
                copy.start()
        shares[5 if layer == 0 else 9].wait_recv()
        arrived(ho_r.at[layer, others], recv_sem.at[layer, HO])
        homes = ho_r[layer].astype(F32)
        homes = jnp.concatenate(
            [homes[:, 8 * g : 8 * g + 8].reshape(half, 128) for g in range(4)], axis=1
        )
        arrived(ll_r.at[layer, others], recv_sem.at[layer, LL])
        levels = ll_r[layer]
        weight = jnp.exp(levels - jnp.max(levels, axis=0, keepdims=True))
        weight = weight / jnp.sum(weight, axis=0, keepdims=True)
        weight = jnp.sum(
            jnp.where(
                iota((n_chip, 16, 128), 1) == iota((n_chip, 16, 128), 2),
                jnp.broadcast_to(weight, (n_chip, 16, 128)),
                0.0,
            ),
            axis=2,
            keepdims=True,
        )
        arrived(lo_r.at[layer, others], recv_sem.at[layer, LO])
        merged = jnp.sum(weight * lo_r[layer].astype(F32), axis=0)
        merged = jnp.concatenate(
            [jnp.where(row16 // 4 == g, merged, 0.0) for g in range(4)], axis=1
        ).astype(BF16)
        attended = (homes + dot(spread[...], merged)).astype(BF16)

        branch = jnp.concatenate(
            [dot(attended, wo[layer, 0]), dot(attended, wo[layer, 1])], axis=1
        )
        zr_s[layer] = branch.astype(BF16).reshape(owners, part, 256)
        for d in z_far:
            remote(
                zr_s.at[layer, lax.rem(z_at[d], owners)], zr_r.at[layer, my_z],
                send_sem.at[layer, ZR], recv_sem.at[layer, ZR], me, z_at[d],
            ).start()
        zr_r[layer, my_z] = zr_s[layer, my_part]
        arrived(zr_r.at[layer, pl.ds(0, nz - 1)], recv_sem.at[layer, ZR])
        hidden = (
            x_half[layer, my_part].astype(F32) + jnp.sum(zr_r[layer].astype(F32), axis=0)
        ).astype(BF16)

        mid = part // 2
        rows_for = {1: (0, part), 7: (0, part), 6: (0, mid), 2: (mid, mid)}
        if layer + 1 < LAYERS:
            za_s[...] = hidden
            x_half[layer + 1, my_part] = hidden
            for d in z_near:
                rows = pl.ds(*rows_for[d])
                remote(
                    za_s.at[rows], x_half.at[layer + 1, my_part, rows],
                    send_sem.at[layer, ZA], recv_sem.at[layer, ZA], me, z_at[d],
                ).start()
            if owners > 1:
                arrived(x_half.at[layer + 1, pl.ds(0, owners - 1)], recv_sem.at[layer, ZA])
        else:
            fin_s[0] = hidden[:, 0:128]
            fin_s[1] = hidden[:, 128:256]
            start = pl.multiple_of(my_part * part, part)
            for d in z_near:
                first, count = rows_for[d]
                rows = pl.ds(first, count)
                to = out.at[core, pl.ds(pl.multiple_of(start + first, count), count)]
                remote(
                    fin_s.at[1, rows], to,
                    send_sem.at[layer, ZB], recv_sem.at[layer, ZB], sib, z_at[d],
                ).start()
                remote(
                    fin_s.at[0, rows], to,
                    send_sem.at[layer, ZA], recv_sem.at[layer, ZA], me, z_at[d],
                ).start()
            to = out.at[core, pl.ds(start, part)]
            remote(
                fin_s.at[1], to,
                send_sem.at[layer, ZB], recv_sem.at[layer, ZB], sib, my_z,
            ).start()
            mine = pltpu.make_async_copy(fin_s.at[0], to, new_sem.at[2])
            mine.start()
            mine.wait()
            for copy in news:
                copy.wait()
            most = pl.ds(0, half - part)
            if owners > 1:
                arrived(out.at[core, most], recv_sem.at[layer, ZA])
            arrived(out.at[1 - core], recv_sem.at[layer, ZB])

    for copy in shares:
        copy.wait_send()
    x_share.wait_send()
    for layer in range(LAYERS):
        for ref, phase in (
            (rs_r.at[layer, others], RS),
            (sq_r.at[layer, others], SQ),
            (rl_r.at[layer, others], RL),
            (sl_r.at[layer, others], SL),
            (px_r.at[layer], PX),
            (ho_r.at[layer, others], HO),
            (lo_r.at[layer, others], LO),
            (ll_r.at[layer, others], LL),
            (zr_r.at[layer, pl.ds(0, nz - 1)], ZR),
        ):
            arrived(ref, send_sem.at[layer, phase])
        if layer + 1 < LAYERS:
            if owners > 1:
                arrived(x_half.at[layer + 1, pl.ds(0, owners - 1)], send_sem.at[layer, ZA])
        else:
            if owners > 1:
                arrived(out.at[core, most], send_sem.at[layer, ZA])
            arrived(out.at[1 - core], send_sem.at[layer, ZB])


def finish(hidden, new_keys, new_values, out, out_keys, out_values, rows, k_rows, v_rows, sem):
    first = [
        pltpu.make_async_copy(hidden.at[0], rows.at[:, 0], sem.at[0]),
        pltpu.make_async_copy(hidden.at[1], rows.at[:, 1], sem.at[1]),
        pltpu.make_async_copy(new_keys, k_rows, sem.at[2]),
        pltpu.make_async_copy(new_values, v_rows, sem.at[3]),
    ]
    last = [
        pltpu.make_async_copy(rows, out, sem.at[4]),
        pltpu.make_async_copy(k_rows, out_keys, sem.at[5]),
        pltpu.make_async_copy(v_rows, out_values, sem.at[6]),
    ]
    for copy in first:
        copy.start()
    first[0].wait()
    first[1].wait()
    last[0].start()
    first[2].wait()
    last[1].start()
    first[3].wait()
    last[2].start()
    for copy in last:
        copy.wait()


def on_device(
    n_chip, side, nz, width,
    hidden_in, norm_gain, q_gain, k_gain, w_query, w_key, w_value, w_out,
    cache_keys, cache_values, lengths, block_owner, block_fill,
):
    half = 8 * n_chip
    owners = nz // 2
    part = half // owners
    blocks = cache_keys.shape[1]
    total = hidden_in.shape[0]
    heads = w_query.shape[2]
    exponent = np.concatenate([np.arange(64), np.arange(64)]) * 2.0 / 128
    frequency = jnp.asarray((THETA**-exponent).astype(np.float32)[None, :])
    vmem, sem = pltpu.VMEM, pltpu.SemaphoreType.DMA
    anywhere = pl.BlockSpec(memory_space=pl.ANY)
    both = (LAYERS, n_chip)
    news = jax.ShapeDtypeStruct((LAYERS, 8, 128), BF16)
    hidden, new_keys, new_values = pl.pallas_call(
        functools.partial(kernel, n_chip, side, nz, float(width)),
        out_shape=(jax.ShapeDtypeStruct((2, half, 128), BF16), news, news),
        in_specs=[anywhere] * 14,
        out_specs=(anywhere, anywhere, anywhere),
        scratch_shapes=[
            vmem((total, 128), BF16),
            vmem((total, 128), BF16),
            vmem((LAYERS, 256), BF16),
            vmem((LAYERS, 128), BF16),
            vmem((LAYERS, 128), BF16),
            vmem((LAYERS, 256, heads), BF16),
            vmem((LAYERS, 256, 128), BF16),
            vmem((LAYERS, 256, 128), BF16),
            vmem((LAYERS, 2, heads, 128), BF16),
            vmem((LAYERS, blocks + 1, 128, 128), BF16),
            vmem((LAYERS, blocks + 1, 128, 128), BF16),
            vmem((1, total), jnp.int32),
            pltpu.SMEM((blocks,), jnp.int32),
            pltpu.SMEM((blocks,), jnp.int32),
            vmem((1, 128), F32),
            vmem((LAYERS, owners, part, 256), BF16),
            vmem((8, (blocks + 1) * 128), F32),
            vmem((8, 9 * 128), F32),
            vmem((8, 128), F32),
            vmem((8, 128), F32),
            vmem((16, 128), F32),
            vmem((16, 128), F32),
            vmem((8, 128), F32),
            vmem((half, 16), BF16),
            vmem((*both, 16, 384), BF16),
            vmem((*both, 16, 384), BF16),
            vmem((LAYERS, 1, 128), F32),
            vmem((*both, 1, 128), F32),
            vmem((LAYERS, 16, 128), BF16),
            vmem((*both, 16, 128), BF16),
            vmem((LAYERS, 1, 128), F32),
            vmem((*both, 1, 128), F32),
            vmem((16, 256), BF16),
            vmem((16, 256), BF16),
            vmem((LAYERS, 32, 128), F32),
            vmem((LAYERS, 32, 128), F32),
            vmem((LAYERS, 32, 128), BF16),
            vmem((*both, 32, 128), BF16),
            vmem((LAYERS, 16, 128), BF16),
            vmem((*both, 16, 128), BF16),
            vmem((LAYERS, 1, 128), F32),
            vmem((*both, 1, 128), F32),
            vmem((LAYERS, owners, part, 256), BF16),
            vmem((LAYERS, nz, part, 256), BF16),
            vmem((part, 256), BF16),
            vmem((2, part, 128), BF16),
            vmem((2, LAYERS, 8, 128), BF16),
            sem((16,)),
            sem((3,)),
            sem((10,)),
            sem((10,)),
            sem((LAYERS, 12)),
            sem((LAYERS, 12)),
        ],
        compiler_params=pltpu.CompilerParams(
            collective_id=0, has_side_effects=True, vmem_limit_bytes=67043328
        ),
        name="attention_layers",
    )(
        hidden_in, norm_gain, q_gain, k_gain, w_query, w_key, w_value, w_out,
        cache_keys, cache_values, lengths.reshape(1, total), block_owner, block_fill, frequency,
    )
    out, new_keys, new_values = pl.pallas_call(
        finish,
        out_shape=(jax.ShapeDtypeStruct((n_chip, 2, 8, 128), BF16), news, news),
        in_specs=[anywhere] * 3,
        out_specs=(anywhere, anywhere, anywhere),
        scratch_shapes=[
            vmem((n_chip, 2, 8, 128), BF16),
            vmem((LAYERS, 8, 128), BF16),
            vmem((LAYERS, 8, 128), BF16),
            sem((7,)),
        ],
        name="finish",
    )(hidden.reshape(2, n_chip, 8, 128), new_keys, new_values)
    return out.reshape(total, 128), new_keys, new_values


def solution(mesh):
    n_req, nz = mesh.shape["req"], mesh.shape["kv"]
    n_chip = n_req // 2
    side = math.isqrt(n_chip)
    in_specs = (
        P(None, "req"),
        P(None, "req"),
        P(),
        P(),
        P(None, "req", "kv"),
        P(None, "req", "kv"),
        P(None, "req", "kv"),
        P(None, "kv", "req"),
        P(None, "req", None, "kv"),
        P(None, "req", None, "kv"),
        P(),
        P("req"),
        P("req"),
    )
    out_specs = (P(None, "req"), P(None, "req", "kv"), P(None, "req", "kv"))
    return jax.shard_map(
        functools.partial(on_device, n_chip, side, nz, 128 * n_req),
        mesh=mesh,
        in_specs=in_specs,
        out_specs=out_specs,
        check_vma=False,
    )
```

time: 69.4 us -> 61.2 us (0.88)
  Pallas kernels: 64.5 us -> 60.4 us
  local copies, waits for them, and re-layouts: 4.02 us -> 0 us
    pallas_call x1, Pallas kernels: 64.5 us -> 58.9 us  [on_device(): pl.pallas_call(functools.partial(kernel, n_chip, side, nz, float(width)),...]
    unnamed x3 -> x0, local copies, waits for them, and re-layouts: 4.02 us -> none
    pallas_call x0 -> x1, Pallas kernels: none -> 1.47 us  [on_device(): pl.pallas_call(finish, out_shape=(jax.ShapeDtypeStruct((n_chip, 2, 8, 128...]
where the time goes in v3:
time: 61.2 us; the launch traced here: 61.1 us
  Pallas kernels  60.4 us (99%)
  between operations  0.64 us (1%)
    pallas_call x1, Pallas kernels, on_device(): pl.pallas_call(functools.partial(kernel, n_chip, side, nz, float(width)),...  58.9 us
    pallas_call x1, Pallas kernels, on_device(): pl.pallas_call(finish, out_shape=(jax.ShapeDtypeStruct((n_chip, 2, 8, 128...  1.47 us

profile of v3, /device:TPU:1, one launch (start us, length us, event | category | flops | bytes accessed | tf_op | source)
XLA Modules:
  0.0 61.1 jit_solution(9617042257911122889)
XLA Ops:
  0.6 58.9 %attention_layers.1 = (bf16[2,128,128]{2,1,0:T(8,128)(2,1)}, bf16[2,8,128]{2,1,0:T(8,128)(2,1)}, bf16[2,8,128]{2,1,0:T(8,128)(2,1)}) custom-call(bf16[256,128]{1,0:T(8,128)(2,1)} %x_in.1, bf16[2,128]{1,0:T(2,128)(2,1)} %norm_gain.1, bf16[2,128]{1,0:T(2,128)(2,1)} %q_gain.1, bf16[2,128]{1,0:T(2,128)(2,1)} %k_gain.1, bf16[2,128,512]{2,1,0:T(8,128)(2,1)} %w_query.1, ...), custom_call_target="tpu_custom_call" | custom-call | tf_op jit(solution)/shard_map/attention_layers/pallas_call | solution.py:591
  59.6 1.5 %finish.1 = (bf16[16,2,8,128]{3,2,1,0:T(8,128)(2,1)}, bf16[2,8,128]{2,1,0:T(8,128)(2,1)}, bf16[2,8,128]{2,1,0:T(8,128)(2,1)}) custom-call(bf16[2,16,8,128]{3,2,1,0:T(8,128)(2,1)} %bitcast.3, bf16[2,8,128]{2,1,0:T(8,128)(2,1)} %get-tuple-element.10.new_keys, bf16[2,8,128]{2,1,0:T(8,128)(2,1)} %get-tuple-element.11.new_values), custom_call_target="tpu_custom_call" | custom-call | tf_op jit(solution)/shard_map/finish/pallas_call | solution.py:659

commit v4 on v3

--- a/solution.py
+++ b/solution.py
@@ -44,10 +44,10 @@
     out, out_keys, out_values,
     x_own, x_sib, gains, q_gains, k_gains, wq, wk, wv, wo, keys, values,
     lens, owner, fill, freq,
-    x_half, long_bias, home_bias, own_cos, own_sin, long_cos, long_sin, own_pick, spread,
+    x_half, long_bias, new_bias, home_bias, own_cos, own_sin, long_cos, long_sin, own_pick, spread,
     rs_s, rs_r, sq_s, sq_r, rl_s, rl_r, sl_s, sl_r, xl_s, xl_r, px_s, px_r,
-    ho_s, ho_r, lo_s, lo_r, ll_s, ll_r, zr_s, zr_r, za_s, fin_s, new_s,
-    load_sem, new_sem, init_send, init_recv, send_sem, recv_sem,
+    ho_s, ho_r, lo_s, lo_r, ll_s, ll_r, zr_s, zr_r, za_s, fin_s,
+    load_sem, init_send, init_recv, send_sem, recv_sem,
 ):
     half = 8 * n_chip
     owners = nz // 2
@@ -159,6 +159,12 @@
     ).astype(BF16)
     long_sel = jnp.concatenate([long_half, jnp.zeros((8, 128), F32)], axis=0).astype(BF16)
     long_sel = long_sel[:, :half]
+    chunk_sel = dot(
+        long_sel,
+        jnp.where(
+            iota((half, part), 0) == my_part * part + iota((half, part), 1), 1.0, 0.0
+        ).astype(BF16),
+    ).astype(BF16)
     long_any = jnp.concatenate([long_hot, jnp.zeros((8, total), F32)], axis=0).astype(BF16)
     long_pick = jnp.where(lane16 == row16 % 4, 1.0, 0.0)
 
@@ -247,6 +253,14 @@
 
     def as_row(column, mask):
         return jnp.sum(jnp.where(mask, column, 0.0), axis=0, keepdims=True)
+
+    def softmax_mean(s, v):
+        top = jnp.maximum(jnp.max(s, axis=1, keepdims=True), CEIL)
+        p = jnp.exp(s - top)
+        den = jnp.sum(p, axis=1, keepdims=True)
+        num = dot(p.astype(BF16), v)
+        level = jnp.where(den > 0.0, top + jnp.log(jnp.maximum(den, TINY)), FLOOR)
+        return num / jnp.maximum(den, TINY), jnp.broadcast_to(level, (16, 128))
 
     logit = 1.0 / math.sqrt(128)
     others = pl.ds(0, n_chip - 1)
@@ -273,21 +287,20 @@
 
     for layer in range(LAYERS):
         x = x_half[layer].reshape(half, 256)
-        if layer == 0:
-            send_long(layer, long_x)
-        else:
-            long_x = dot(long_sel, x)
-            xl_s[...] = long_x.astype(BF16)
-            x_share = to_sib(xl_s, xl_r, XL, layer)
+        if layer == 1:
+            for at in (6, 7, 8):
+                shares[at].wait_recv()
+            theirs = jnp.sum(xl_r[...].astype(F32), axis=0)
+            long_x = dot(long_sel, x) + jnp.concatenate(
+                [theirs[:, 128:256], theirs[:, 0:128]], axis=1
+            )
+        send_long(layer, long_x)
         x = x.astype(F32)
         square = jnp.sum(x * x, axis=1, keepdims=True)
         square_row = as_row(square, on_diagonal)
         sq_s[layer] = square_row
         sq_r[layer, chip] = square_row
         xg = (x * gains[pl.ds(layer, 1), :].astype(F32)).astype(BF16)
-        if layer == 1:
-            for at in (6, 7, 8):
-                shares[at].wait_recv()
         q = dot(xg, wq[layer])
         upper = q[:, 0:384].reshape(n_chip, 8, 384)
         lower = jnp.concatenate(
@@ -316,7 +329,7 @@
             lax.fori_loop(0, blocks, block_masks, 0)
             live = (long_id == (8 * me + lane8).astype(F32)) & (lane8 < 8) & (sub8 < 4)
             bias = jnp.where(live, 0.0, FLOOR)
-            long_bias[:, pl.ds(blocks * 128, 128)] = twice([bias, bias])
+            new_bias[...] = twice([bias, bias])
             for b in range(8):
                 home_bias[:, pl.ds(b * 128, 128)] = jnp.where(
                     (sub8 == b) & (lane8 < fill[b]), 0.0, FLOOR
@@ -328,14 +341,27 @@
             loads[11].wait()
             loads[12].wait()
         else:
-            x_share.wait_recv()
-            theirs = xl_r[...].astype(F32)
-            send_long(
-                layer,
-                long_x + jnp.concatenate([theirs[:, 128:256], theirs[:, 0:128]], axis=1),
-            )
             loads[14].wait()
             loads[15].wait()
+
+        q_gain_row = q_gains[pl.ds(layer, 1), :].astype(F32)
+        arrived(sl_r.at[layer, others], recv_sem.at[layer, SL])
+        arrived(rl_r.at[layer, others], recv_sem.at[layer, RL])
+        scale = lax.rsqrt(
+            jnp.sum(long_pick * jnp.sum(sl_r[layer], axis=0), axis=1, keepdims=True) / width
+            + EPS
+        )
+        q_long = normed_turned(
+            jnp.sum(rl_r[layer].astype(F32), axis=0) * scale,
+            q_gain_row,
+            long_cos[...],
+            long_sin[...],
+        ).astype(BF16)
+        s = dot_nt(q_long, keys[layer, 0:blocks].reshape(blocks * 128, 128))
+        s = s * logit + jnp.concatenate([long_bias[...]] * 2, axis=0)
+        mean, level = softmax_mean(s, values[layer, 0:blocks].reshape(blocks * 128, 128))
+        px_s[layer] = jnp.concatenate([mean, level], axis=0)
+        p_share = to_sib(px_s.at[layer], px_r.at[layer], PX, layer)
 
         arrived(sq_r.at[layer, others], recv_sem.at[layer, SQ])
         arrived(rs_r.at[layer, others], recv_sem.at[layer, RS])
@@ -344,7 +370,6 @@
             jnp.sum(own_pick[...] * jnp.sum(sq_r[layer], axis=0), axis=1, keepdims=True) / width
             + EPS
         )
-        q_gain_row = q_gains[pl.ds(layer, 1), :].astype(F32)
         new_key = normed_turned(
             sums[8:16, 128:256] * scale,
             k_gains[pl.ds(layer, 1), :].astype(F32),
@@ -355,8 +380,8 @@
         pad = jnp.zeros((8, 128), F32)
         keys[layer, blocks, 0:16] = jnp.concatenate([new_key, pad], axis=0).astype(BF16)
         values[layer, blocks, 0:16] = jnp.concatenate([new_value, pad], axis=0).astype(BF16)
-        new_s[0, layer] = new_key.astype(BF16)
-        new_s[1, layer] = new_value.astype(BF16)
+        out_keys[layer] = new_key.astype(BF16)
+        out_values[layer] = new_value.astype(BF16)
         q_own = [
             normed_turned(t * scale, q_gain_row, own_cos[...], own_sin[...])
             for t in (
@@ -365,29 +390,9 @@
         ]
         q_own = jnp.concatenate(q_own, axis=0).astype(BF16)
 
-        arrived(sl_r.at[layer, others], recv_sem.at[layer, SL])
-        arrived(rl_r.at[layer, others], recv_sem.at[layer, RL])
-        scale = lax.rsqrt(
-            jnp.sum(long_pick * jnp.sum(sl_r[layer], axis=0), axis=1, keepdims=True) / width
-            + EPS
-        )
-        q_long = normed_turned(
-            jnp.sum(rl_r[layer].astype(F32), axis=0) * scale,
-            q_gain_row,
-            long_cos[...],
-            long_sin[...],
-        ).astype(BF16)
-        s = dot_nt(q_long, keys[layer].reshape((blocks + 1) * 128, 128))
-        s = s * logit + jnp.concatenate([long_bias[...]] * 2, axis=0)
-        top = jnp.maximum(jnp.max(s, axis=1, keepdims=True), CEIL)
-        p = jnp.exp(s - top)
-        den = jnp.sum(p, axis=1, keepdims=True)
-        num = dot(p.astype(BF16), values[layer].reshape((blocks + 1) * 128, 128))
-        level = jnp.where(den > 0.0, top + jnp.log(jnp.maximum(den, TINY)), FLOOR)
-        level = jnp.broadcast_to(level, (16, 128))
-        mean = num / jnp.maximum(den, TINY)
-        px_s[layer] = jnp.concatenate([mean, level], axis=0)
-        p_share = to_sib(px_s.at[layer], px_r.at[layer], PX, layer)
+        s = dot_nt(q_long, keys[layer, blocks])
+        s = s * logit + jnp.concatenate([new_bias[...]] * 2, axis=0)
+        new_mean, new_level = softmax_mean(s, values[layer, blocks])
 
         s = jnp.concatenate(
             [
@@ -410,11 +415,12 @@
 
         p_share.wait_recv()
         other_mean, other_level = px_r[layer, 0:16], px_r[layer, 16:32]
-        top = jnp.maximum(level, other_level)
-        mine, theirs = jnp.exp(level - top), jnp.exp(other_level - top)
-        both = mine + theirs
-        mean = ((mean * mine + other_mean * theirs) / both).astype(BF16)
-        level_row = as_row(top + jnp.log(both), row16 == lane16)
+        top = jnp.maximum(jnp.maximum(level, new_level), other_level)
+        mine, fresh = jnp.exp(level - top), jnp.exp(new_level - top)
+        theirs = jnp.exp(other_level - top)
+        every = mine + fresh + theirs
+        mean = ((mean * mine + new_mean * fresh + other_mean * theirs) / every).astype(BF16)
+        level_row = as_row(top + jnp.log(every), row16 == lane16)
         lo_s[layer] = mean
         lo_r[layer, chip] = mean
         ll_s[layer] = level_row
@@ -429,13 +435,6 @@
 
         if layer == 0:
             loads[13].wait()
-        else:
-            news = [
-                pltpu.make_async_copy(new_s.at[at], ref, new_sem.at[at])
-                for at, ref in enumerate((out_keys, out_values))
-            ]
-            for copy in news:
-                copy.start()
         shares[5 if layer == 0 else 9].wait_recv()
         arrived(ho_r.at[layer, others], recv_sem.at[layer, HO])
         homes = ho_r[layer].astype(F32)
@@ -482,14 +481,25 @@
         if layer + 1 < LAYERS:
             za_s[...] = hidden
             x_half[layer + 1, my_part] = hidden
+            xl_s[...] = dot(chunk_sel, hidden).astype(BF16)
             for d in z_near:
+                if d != 6:
+                    remote(
+                        xl_s, xl_r.at[my_part],
+                        send_sem.at[layer, XL], recv_sem.at[layer, XL], sib, z_at[d],
+                    ).start()
                 rows = pl.ds(*rows_for[d])
                 remote(
                     za_s.at[rows], x_half.at[layer + 1, my_part, rows],
                     send_sem.at[layer, ZA], recv_sem.at[layer, ZA], me, z_at[d],
                 ).start()
+            remote(
+                xl_s, xl_r.at[my_part],
+                send_sem.at[layer, XL], recv_sem.at[layer, XL], sib, my_z,
+            ).start()
             if owners > 1:
                 arrived(x_half.at[layer + 1, pl.ds(0, owners - 1)], recv_sem.at[layer, ZA])
+            arrived(xl_r, recv_sem.at[layer, XL])
         else:
             fin_s[0] = hidden[:, 0:128]
             fin_s[1] = hidden[:, 128:256]
@@ -511,11 +521,7 @@
                 fin_s.at[1], to,
                 send_sem.at[layer, ZB], recv_sem.at[layer, ZB], sib, my_z,
             ).start()
-            mine = pltpu.make_async_copy(fin_s.at[0], to, new_sem.at[2])
-            mine.start()
-            mine.wait()
-            for copy in news:
-                copy.wait()
+            out[core, pl.ds(start, part)] = hidden[:, 0:128]
             most = pl.ds(0, half - part)
             if owners > 1:
                 arrived(out.at[core, most], recv_sem.at[layer, ZA])
@@ -523,7 +529,6 @@
 
     for copy in shares:
         copy.wait_send()
-    x_share.wait_send()
     for layer in range(LAYERS):
         for ref, phase in (
             (rs_r.at[layer, others], RS),
@@ -538,6 +543,7 @@
         ):
             arrived(ref, send_sem.at[layer, phase])
         if layer + 1 < LAYERS:
+            arrived(xl_r, send_sem.at[layer, XL])
             if owners > 1:
                 arrived(x_half.at[layer + 1, pl.ds(0, owners - 1)], send_sem.at[layer, ZA])
         else:
@@ -546,28 +552,16 @@
             arrived(out.at[1 - core], send_sem.at[layer, ZB])
 
 
-def finish(hidden, new_keys, new_values, out, out_keys, out_values, rows, k_rows, v_rows, sem):
-    first = [
-        pltpu.make_async_copy(hidden.at[0], rows.at[:, 0], sem.at[0]),
-        pltpu.make_async_copy(hidden.at[1], rows.at[:, 1], sem.at[1]),
-        pltpu.make_async_copy(new_keys, k_rows, sem.at[2]),
-        pltpu.make_async_copy(new_values, v_rows, sem.at[3]),
+def finish(hidden, new_keys, new_values, out, out_keys, out_values, sem):
+    copies = [
+        pltpu.make_async_copy(hidden.at[0], out.at[:, 0], sem.at[0]),
+        pltpu.make_async_copy(hidden.at[1], out.at[:, 1], sem.at[1]),
+        pltpu.make_async_copy(new_keys, out_keys, sem.at[2]),
+        pltpu.make_async_copy(new_values, out_values, sem.at[3]),
     ]
-    last = [
-        pltpu.make_async_copy(rows, out, sem.at[4]),
-        pltpu.make_async_copy(k_rows, out_keys, sem.at[5]),
-        pltpu.make_async_copy(v_rows, out_values, sem.at[6]),
-    ]
-    for copy in first:
+    for copy in copies:
         copy.start()
-    first[0].wait()
-    first[1].wait()
-    last[0].start()
-    first[2].wait()
-    last[1].start()
-    first[3].wait()
-    last[2].start()
-    for copy in last:
+    for copy in copies:
         copy.wait()
 
 
@@ -587,12 +581,14 @@
     vmem, sem = pltpu.VMEM, pltpu.SemaphoreType.DMA
     anywhere = pl.BlockSpec(memory_space=pl.ANY)
     both = (LAYERS, n_chip)
+    onchip = pl.BlockSpec(memory_space=pltpu.VMEM)
     news = jax.ShapeDtypeStruct((LAYERS, 8, 128), BF16)
+    chip_news = vmem((LAYERS, 8, 128), BF16)
     hidden, new_keys, new_values = pl.pallas_call(
         functools.partial(kernel, n_chip, side, nz, float(width)),
-        out_shape=(jax.ShapeDtypeStruct((2, half, 128), BF16), news, news),
+        out_shape=(vmem((2, half, 128), BF16), chip_news, chip_news),
         in_specs=[anywhere] * 14,
-        out_specs=(anywhere, anywhere, anywhere),
+        out_specs=(onchip, onchip, onchip),
         scratch_shapes=[
             vmem((total, 128), BF16),
             vmem((total, 128), BF16),
@@ -610,7 +606,8 @@
             pltpu.SMEM((blocks,), jnp.int32),
             vmem((1, 128), F32),
             vmem((LAYERS, owners, part, 256), BF16),
-            vmem((8, (blocks + 1) * 128), F32),
+            vmem((8, blocks * 128), F32),
+            vmem((8, 128), F32),
             vmem((8, 9 * 128), F32),
             vmem((8, 128), F32),
             vmem((8, 128), F32),
@@ -627,7 +624,7 @@
             vmem((LAYERS, 1, 128), F32),
             vmem((*both, 1, 128), F32),
             vmem((16, 256), BF16),
-            vmem((16, 256), BF16),
+            vmem((owners, 16, 256), BF16),
             vmem((LAYERS, 32, 128), F32),
             vmem((LAYERS, 32, 128), F32),
             vmem((LAYERS, 32, 128), BF16),
@@ -640,16 +637,14 @@
             vmem((LAYERS, nz, part, 256), BF16),
             vmem((part, 256), BF16),
             vmem((2, part, 128), BF16),
-            vmem((2, LAYERS, 8, 128), BF16),
             sem((16,)),
-            sem((3,)),
             sem((10,)),
             sem((10,)),
             sem((LAYERS, 12)),
             sem((LAYERS, 12)),
         ],
         compiler_params=pltpu.CompilerParams(
-            collective_id=0, has_side_effects=True, vmem_limit_bytes=67043328
+            collective_id=0, has_side_effects=True, vmem_limit_bytes=60000 * 1024
         ),
         name="attention_layers",
     )(
@@ -659,14 +654,10 @@
     out, new_keys, new_values = pl.pallas_call(
         finish,
         out_shape=(jax.ShapeDtypeStruct((n_chip, 2, 8, 128), BF16), news, news),
-        in_specs=[anywhere] * 3,
+        in_specs=[onchip] * 3,
         out_specs=(anywhere, anywhere, anywhere),
-        scratch_shapes=[
-            vmem((n_chip, 2, 8, 128), BF16),
-            vmem((LAYERS, 8, 128), BF16),
-            vmem((LAYERS, 8, 128), BF16),
-            sem((7,)),
-        ],
+        scratch_shapes=[sem((4,))],
+        compiler_params=pltpu.CompilerParams(vmem_limit_bytes=1024 * 1024),
         name="finish",
     )(hidden.reshape(2, n_chip, 8, 128), new_keys, new_values)
     return out.reshape(total, 128), new_keys, new_values

time: 61.2 us -> 58.1 us (0.949)
  Pallas kernels: 60.4 us -> 57.4 us
    pallas_call x1, Pallas kernels: 58.9 us -> 56.7 us  [on_device(): pl.pallas_call(functools.partial(kernel, n_chip, side, nz, float(width)),...]
    pallas_call x1, Pallas kernels: 1.47 us -> 0.67 us  [on_device(): pl.pallas_call(finish, out_shape=(jax.ShapeDtypeStruct((n_chip, 2, 8, 128...]
where the time goes in v4:
time: 58.1 us; the launch traced here: 58 us
  Pallas kernels  57.4 us (99%)
  between operations  0.64 us (1%)
    pallas_call x1, Pallas kernels, on_device(): pl.pallas_call(functools.partial(kernel, n_chip, side, nz, float(width)),...  56.7 us

profile of v4, /device:TPU:1, one launch (start us, length us, event | category | flops | bytes accessed | tf_op | source)
XLA Modules:
  0.0 58.0 jit_solution(11125002840046508403)
XLA Ops:
  0.6 56.7 %attention_layers.1 = (bf16[2,128,128]{2,1,0:T(8,128)(2,1)S(1)}, bf16[2,8,128]{2,1,0:T(8,128)(2,1)S(1)}, bf16[2,8,128]{2,1,0:T(8,128)(2,1)S(1)}) custom-call(bf16[256,128]{1,0:T(8,128)(2,1)} %x_in.1, bf16[2,128]{1,0:T(2,128)(2,1)} %norm_gain.1, bf16[2,128]{1,0:T(2,128)(2,1)} %q_gain.1, bf16[2,128]{1,0:T(2,128)(2,1)} %k_gain.1, bf16[2,128,512]{2,1,0:T(8,128)(2,1)} %w_query.1, ...), custom_call_target="tpu_custom_call" | custom-call | tf_op jit(solution)/shard_map/attention_layers/pallas_call | solution.py:587
  57.4 0.7 %finish.1 = (bf16[16,2,8,128]{3,2,1,0:T(8,128)(2,1)}, bf16[2,8,128]{2,1,0:T(8,128)(2,1)}, bf16[2,8,128]{2,1,0:T(8,128)(2,1)}) custom-call(bf16[2,16,8,128]{3,2,1,0:T(8,128)(2,1)S(1)} %bitcast.3, bf16[2,8,128]{2,1,0:T(8,128)(2,1)S(1)} %get-tuple-element.10.new_keys, bf16[2,8,128]{2,1,0:T(8,128)(2,1)S(1)} %get-tuple-element.11.new_values), custom_call_target="tpu_custom_call" | custom-call | tf_op jit(solution)/shard_map/finish/pallas_call | solution.py:654

commit v5 on v4

--- a/solution.py
+++ b/solution.py
@@ -19,7 +19,7 @@
 F32 = jnp.float32
 BF16 = jnp.bfloat16
 
-RS, SQ, RL, SL, XL, PX, HO, LO, LL, ZR, ZA, ZB = range(12)
+RS, SQ, RL, SL, LZ, LW, PX, HO, LL, ZR, ZA, ZB = range(12)
 
 
 def dot(a, b):
@@ -45,8 +45,8 @@
     x_own, x_sib, gains, q_gains, k_gains, wq, wk, wv, wo, keys, values,
     lens, owner, fill, freq,
     x_half, long_bias, new_bias, home_bias, own_cos, own_sin, long_cos, long_sin, own_pick, spread,
-    rs_s, rs_r, sq_s, sq_r, rl_s, rl_r, sl_s, sl_r, xl_s, xl_r, px_s, px_r,
-    ho_s, ho_r, lo_s, lo_r, ll_s, ll_r, zr_s, zr_r, za_s, fin_s,
+    rs_s, rs_r, sq_s, sq_r, rl_s, rl_r, sl_s, sl_r, lz_s, lz_r, px_s, px_r,
+    ho_s, ho_r, ll_s, ll_r, zr_s, zr_r, za_s, fin_s,
     load_sem, init_send, init_recv, send_sem, recv_sem,
 ):
     half = 8 * n_chip
@@ -88,7 +88,6 @@
         greet(req, my_z)
     for d in z_far:
         greet(me, z_at[d])
-    for d in z_near:
         greet(sib, z_at[d])
     greet(sib, my_z)
 
@@ -159,12 +158,6 @@
     ).astype(BF16)
     long_sel = jnp.concatenate([long_half, jnp.zeros((8, 128), F32)], axis=0).astype(BF16)
     long_sel = long_sel[:, :half]
-    chunk_sel = dot(
-        long_sel,
-        jnp.where(
-            iota((half, part), 0) == my_part * part + iota((half, part), 1), 1.0, 0.0
-        ).astype(BF16),
-    ).astype(BF16)
     long_any = jnp.concatenate([long_hot, jnp.zeros((8, total), F32)], axis=0).astype(BF16)
     long_pick = jnp.where(lane16 == row16 % 4, 1.0, 0.0)
 
@@ -187,7 +180,7 @@
     x_first = half_of(x_own)
     long_first = dot(long_any, x_own[...])
 
-    pl.semaphore_wait(barrier, len(peers) + len(z_far) + len(z_near) + 1)
+    pl.semaphore_wait(barrier, len(peers) + 2 * len(z_far) + 1)
 
     def remote(src, dst, send, recv, req, kv):
         return pltpu.make_async_remote_copy(
@@ -287,14 +280,8 @@
 
     for layer in range(LAYERS):
         x = x_half[layer].reshape(half, 256)
-        if layer == 1:
-            for at in (6, 7, 8):
-                shares[at].wait_recv()
-            theirs = jnp.sum(xl_r[...].astype(F32), axis=0)
-            long_x = dot(long_sel, x) + jnp.concatenate(
-                [theirs[:, 128:256], theirs[:, 0:128]], axis=1
-            )
-        send_long(layer, long_x)
+        if layer == 0:
+            send_long(layer, long_x)
         x = x.astype(F32)
         square = jnp.sum(x * x, axis=1, keepdims=True)
         square_row = as_row(square, on_diagonal)
@@ -409,9 +396,8 @@
             p[:, 1024:1152], values[layer, blocks]
         )
         attended = (num * (jnp.concatenate([own_keep] * 4, axis=0) / den)).astype(BF16)
-        ho_s[layer] = attended
-        ho_r[layer, chip] = attended
-        to_chips(lambda to: [(ho_s.at[layer], ho_r.at[layer, chip], HO)], layer)
+        ho_s[layer, 0:32] = attended
+        ho_r[layer, chip, 0:32] = attended
 
         p_share.wait_recv()
         other_mean, other_level = px_r[layer, 0:16], px_r[layer, 16:32]
@@ -421,13 +407,13 @@
         every = mine + fresh + theirs
         mean = ((mean * mine + new_mean * fresh + other_mean * theirs) / every).astype(BF16)
         level_row = as_row(top + jnp.log(every), row16 == lane16)
-        lo_s[layer] = mean
-        lo_r[layer, chip] = mean
+        ho_s[layer, 32:48] = mean
+        ho_r[layer, chip, 32:48] = mean
         ll_s[layer] = level_row
         ll_r[layer, chip] = level_row
         to_chips(
             lambda to: [
-                (lo_s.at[layer], lo_r.at[layer, chip], LO),
+                (ho_s.at[layer], ho_r.at[layer, chip], HO),
                 (ll_s.at[layer], ll_r.at[layer, chip], LL),
             ],
             layer,
@@ -437,7 +423,7 @@
             loads[13].wait()
         shares[5 if layer == 0 else 9].wait_recv()
         arrived(ho_r.at[layer, others], recv_sem.at[layer, HO])
-        homes = ho_r[layer].astype(F32)
+        homes = ho_r[layer, :, 0:32].astype(F32)
         homes = jnp.concatenate(
             [homes[:, 8 * g : 8 * g + 8].reshape(half, 128) for g in range(4)], axis=1
         )
@@ -454,8 +440,7 @@
             axis=2,
             keepdims=True,
         )
-        arrived(lo_r.at[layer, others], recv_sem.at[layer, LO])
-        merged = jnp.sum(weight * lo_r[layer].astype(F32), axis=0)
+        merged = jnp.sum(weight * ho_r[layer, :, 32:48].astype(F32), axis=0)
         merged = jnp.concatenate(
             [jnp.where(row16 // 4 == g, merged, 0.0) for g in range(4)], axis=1
         ).astype(BF16)
@@ -464,11 +449,30 @@
         branch = jnp.concatenate(
             [dot(attended, wo[layer, 0]), dot(attended, wo[layer, 1])], axis=1
         )
-        zr_s[layer] = branch.astype(BF16).reshape(owners, part, 256)
+        branch = branch.astype(BF16)
+        zr_s[layer] = branch.reshape(owners, part, 256)
+        if layer + 1 < LAYERS:
+            long_branch = dot(long_sel, branch).astype(BF16)
+            lz_s[...] = long_branch
+            lz_r[0, my_z] = long_branch
         for d in z_far:
             remote(
                 zr_s.at[layer, lax.rem(z_at[d], owners)], zr_r.at[layer, my_z],
                 send_sem.at[layer, ZR], recv_sem.at[layer, ZR], me, z_at[d],
+            ).start()
+        if layer + 1 < LAYERS:
+            for d in z_far:
+                remote(
+                    lz_s, lz_r.at[0, my_z],
+                    send_sem.at[layer, LZ], recv_sem.at[layer, LZ], me, z_at[d],
+                ).start()
+                remote(
+                    lz_s, lz_r.at[1, my_z],
+                    send_sem.at[layer, LW], recv_sem.at[layer, LW], sib, z_at[d],
+                ).start()
+            remote(
+                lz_s, lz_r.at[1, my_z],
+                send_sem.at[layer, LW], recv_sem.at[layer, LW], sib, my_z,
             ).start()
         zr_r[layer, my_z] = zr_s[layer, my_part]
         arrived(zr_r.at[layer, pl.ds(0, nz - 1)], recv_sem.at[layer, ZR])
@@ -481,25 +485,24 @@
         if layer + 1 < LAYERS:
             za_s[...] = hidden
             x_half[layer + 1, my_part] = hidden
-            xl_s[...] = dot(chunk_sel, hidden).astype(BF16)
             for d in z_near:
-                if d != 6:
-                    remote(
-                        xl_s, xl_r.at[my_part],
-                        send_sem.at[layer, XL], recv_sem.at[layer, XL], sib, z_at[d],
-                    ).start()
                 rows = pl.ds(*rows_for[d])
                 remote(
                     za_s.at[rows], x_half.at[layer + 1, my_part, rows],
                     send_sem.at[layer, ZA], recv_sem.at[layer, ZA], me, z_at[d],
                 ).start()
-            remote(
-                xl_s, xl_r.at[my_part],
-                send_sem.at[layer, XL], recv_sem.at[layer, XL], sib, my_z,
-            ).start()
+            arrived(lz_r.at[0, pl.ds(0, nz - 1)], recv_sem.at[layer, LZ])
+            arrived(lz_r.at[1], recv_sem.at[layer, LW])
+            theirs = jnp.sum(lz_r[1].astype(F32), axis=0)
+            long_x = long_x + (
+                jnp.sum(lz_r[0].astype(F32), axis=0)
+                + jnp.concatenate([theirs[:, 128:256], theirs[:, 0:128]], axis=1)
+            )
+            for at in (6, 7, 8):
+                shares[at].wait_recv()
+            send_long(layer + 1, long_x.astype(BF16).astype(F32))
             if owners > 1:
                 arrived(x_half.at[layer + 1, pl.ds(0, owners - 1)], recv_sem.at[layer, ZA])
-            arrived(xl_r, recv_sem.at[layer, XL])
         else:
             fin_s[0] = hidden[:, 0:128]
             fin_s[1] = hidden[:, 128:256]
@@ -537,13 +540,13 @@
             (sl_r.at[layer, others], SL),
             (px_r.at[layer], PX),
             (ho_r.at[layer, others], HO),
-            (lo_r.at[layer, others], LO),
             (ll_r.at[layer, others], LL),
             (zr_r.at[layer, pl.ds(0, nz - 1)], ZR),
         ):
             arrived(ref, send_sem.at[layer, phase])
         if layer + 1 < LAYERS:
-            arrived(xl_r, send_sem.at[layer, XL])
+            arrived(lz_r.at[0, pl.ds(0, nz - 1)], send_sem.at[layer, LZ])
+            arrived(lz_r.at[1], send_sem.at[layer, LW])
             if owners > 1:
                 arrived(x_half.at[layer + 1, pl.ds(0, owners - 1)], send_sem.at[layer, ZA])
         else:
@@ -624,13 +627,11 @@
             vmem((LAYERS, 1, 128), F32),
             vmem((*both, 1, 128), F32),
             vmem((16, 256), BF16),
-            vmem((owners, 16, 256), BF16),
+            vmem((2, nz, 16, 256), BF16),
             vmem((LAYERS, 32, 128), F32),
             vmem((LAYERS, 32, 128), F32),
-            vmem((LAYERS, 32, 128), BF16),
-            vmem((*both, 32, 128), BF16),
-            vmem((LAYERS, 16, 128), BF16),
-            vmem((*both, 16, 128), BF16),
+            vmem((LAYERS, 48, 128), BF16),
+            vmem((*both, 48, 128), BF16),
             vmem((LAYERS, 1, 128), F32),
             vmem((*both, 1, 128), F32),
             vmem((LAYERS, owners, part, 256), BF16),

time: 58.1 us -> 57.8 us (level)
  no operation moved by 1% of the time
where the time goes in v5:
time: 57.8 us; the launch traced here: 57.7 us
  Pallas kernels  57.1 us (99%)
  between operations  0.64 us (1%)
    pallas_call x1, Pallas kernels, on_device(): pl.pallas_call(functools.partial(kernel, n_chip, side, nz, float(width)),...  56.4 us

profile of v5, /device:TPU:1, one launch (start us, length us, event | category | flops | bytes accessed | tf_op | source)
XLA Modules:
  0.0 57.7 jit_solution(1851686613071070222)
XLA Ops:
  0.6 56.4 %attention_layers.1 = (bf16[2,128,128]{2,1,0:T(8,128)(2,1)S(1)}, bf16[2,8,128]{2,1,0:T(8,128)(2,1)S(1)}, bf16[2,8,128]{2,1,0:T(8,128)(2,1)S(1)}) custom-call(bf16[256,128]{1,0:T(8,128)(2,1)} %x_in.1, bf16[2,128]{1,0:T(2,128)(2,1)} %norm_gain.1, bf16[2,128]{1,0:T(2,128)(2,1)} %q_gain.1, bf16[2,128]{1,0:T(2,128)(2,1)} %k_gain.1, bf16[2,128,512]{2,1,0:T(8,128)(2,1)} %w_query.1, ...), custom_call_target="tpu_custom_call" | custom-call | tf_op jit(solution)/shard_map/attention_layers/pallas_call | solution.py:590
  57.0 0.7 %finish.1 = (bf16[16,2,8,128]{3,2,1,0:T(8,128)(2,1)}, bf16[2,8,128]{2,1,0:T(8,128)(2,1)}, bf16[2,8,128]{2,1,0:T(8,128)(2,1)}) custom-call(bf16[2,16,8,128]{3,2,1,0:T(8,128)(2,1)S(1)} %bitcast.3, bf16[2,8,128]{2,1,0:T(8,128)(2,1)S(1)} %get-tuple-element.10.new_keys, bf16[2,8,128]{2,1,0:T(8,128)(2,1)S(1)} %get-tuple-element.11.new_values), custom_call_target="tpu_custom_call" | custom-call | tf_op jit(solution)/shard_map/finish/pallas_call | solution.py:655

commit v6 on v5

--- a/solution.py
+++ b/solution.py
@@ -452,7 +452,8 @@
         branch = branch.astype(BF16)
         zr_s[layer] = branch.reshape(owners, part, 256)
         if layer + 1 < LAYERS:
-            long_branch = dot(long_sel, branch).astype(BF16)
+            long_branch = dot(long_sel, branch)[0:8]
+            long_branch = twice([long_branch[:, 0:128], long_branch[:, 128:256]]).astype(BF16)
             lz_s[...] = long_branch
             lz_r[0, my_z] = long_branch
         for d in z_far:
@@ -493,11 +494,13 @@
                 ).start()
             arrived(lz_r.at[0, pl.ds(0, nz - 1)], recv_sem.at[layer, LZ])
             arrived(lz_r.at[1], recv_sem.at[layer, LW])
+            mine = jnp.sum(lz_r[0].astype(F32), axis=0)
             theirs = jnp.sum(lz_r[1].astype(F32), axis=0)
-            long_x = long_x + (
-                jnp.sum(lz_r[0].astype(F32), axis=0)
-                + jnp.concatenate([theirs[:, 128:256], theirs[:, 0:128]], axis=1)
-            )
+            far = pltpu.roll(theirs, 4, 0)
+            near = pltpu.roll(mine, 4, 0)
+            gained = jnp.concatenate([mine + far, near + theirs], axis=1)
+            gained = jnp.where(iota((8, 256), 0) < 4, gained, 0.0)
+            long_x = long_x + jnp.concatenate([gained, jnp.zeros((8, 256), F32)], axis=0)
             for at in (6, 7, 8):
                 shares[at].wait_recv()
             send_long(layer + 1, long_x.astype(BF16).astype(F32))
@@ -626,8 +629,8 @@
             vmem((*both, 16, 128), BF16),
             vmem((LAYERS, 1, 128), F32),
             vmem((*both, 1, 128), F32),
-            vmem((16, 256), BF16),
-            vmem((2, nz, 16, 256), BF16),
+            vmem((8, 128), BF16),
+            vmem((2, nz, 8, 128), BF16),
             vmem((LAYERS, 32, 128), F32),
             vmem((LAYERS, 32, 128), F32),
             vmem((LAYERS, 48, 128), BF16),

time: 57.8 us -> 56.8 us (0.983)
  Pallas kernels: 57.1 us -> 56 us
    pallas_call x1, Pallas kernels: 56.4 us -> 55.4 us  [on_device(): pl.pallas_call(functools.partial(kernel, n_chip, side, nz, float(width)),...]
where the time goes in v6:
time: 56.8 us; the launch traced here: 56.7 us
  Pallas kernels  56 us (99%)
  between operations  0.64 us (1%)
    pallas_call x1, Pallas kernels, on_device(): pl.pallas_call(functools.partial(kernel, n_chip, side, nz, float(width)),...  55.4 us

profile of v6, /device:TPU:1, one launch (start us, length us, event | category | flops | bytes accessed | tf_op | source)
XLA Modules:
  0.0 56.7 jit_solution(8776566631365819910)
XLA Ops:
  0.6 55.4 %attention_layers.1 = (bf16[2,128,128]{2,1,0:T(8,128)(2,1)S(1)}, bf16[2,8,128]{2,1,0:T(8,128)(2,1)S(1)}, bf16[2,8,128]{2,1,0:T(8,128)(2,1)S(1)}) custom-call(bf16[256,128]{1,0:T(8,128)(2,1)} %x_in.1, bf16[2,128]{1,0:T(2,128)(2,1)} %norm_gain.1, bf16[2,128]{1,0:T(2,128)(2,1)} %q_gain.1, bf16[2,128]{1,0:T(2,128)(2,1)} %k_gain.1, bf16[2,128,512]{2,1,0:T(8,128)(2,1)} %w_query.1, ...), custom_call_target="tpu_custom_call" | custom-call | tf_op jit(solution)/shard_map/attention_layers/pallas_call | solution.py:593
  56.0 0.7 %finish.1 = (bf16[16,2,8,128]{3,2,1,0:T(8,128)(2,1)}, bf16[2,8,128]{2,1,0:T(8,128)(2,1)}, bf16[2,8,128]{2,1,0:T(8,128)(2,1)}) custom-call(bf16[2,16,8,128]{3,2,1,0:T(8,128)(2,1)S(1)} %bitcast.3, bf16[2,8,128]{2,1,0:T(8,128)(2,1)S(1)} %get-tuple-element.10.new_keys, bf16[2,8,128]{2,1,0:T(8,128)(2,1)S(1)} %get-tuple-element.11.new_values), custom_call_target="tpu_custom_call" | custom-call | tf_op jit(solution)/shard_map/finish/pallas_call | solution.py:658

commit v7 on v6

--- a/solution.py
+++ b/solution.py
@@ -73,6 +73,7 @@
     at_y = [lax.rem(chip_y + d, side) for d in range(side)]
     chips = [at_x[dx] + at_y[dy] for dx, dy in steps]
     peers = [2 * c + core for c in chips]
+    strangers = [2 * c + 1 - core for c in chips] + [sib]
     z_at = [lax.rem(my_z + d, nz) for d in range(nz)]
     z_far = sorted(range(1, nz), key=lambda d: -ring(d, nz))
     z_near = {8: (6, 2, 7, 1), 2: ()}[nz]
@@ -84,12 +85,11 @@
             barrier, inc=1, device_id={"req": req, "kv": kv}, device_id_type=MESH
         )
 
-    for req in peers:
+    for req in peers + strangers:
         greet(req, my_z)
     for d in z_far:
         greet(me, z_at[d])
         greet(sib, z_at[d])
-    greet(sib, my_z)
 
     loads = [
         pltpu.make_async_copy(src, dst, load_sem.at[at])
@@ -180,7 +180,26 @@
     x_first = half_of(x_own)
     long_first = dot(long_any, x_own[...])
 
-    pl.semaphore_wait(barrier, len(peers) + 2 * len(z_far) + 1)
+    def as_row(column, mask):
+        return jnp.sum(jnp.where(mask, column, 0.0), axis=0, keepdims=True)
+
+    def long_message(layer, rows, columns, slot):
+        square = jnp.sum(rows * rows, axis=1, keepdims=True)
+        square_row = as_row(square, row16 == lane16)
+        sl_s[layer] = square_row
+        sl_r[layer, slot] = square_row
+        gain = gains[pl.ds(layer, 1), 0:columns].astype(F32)
+        q = dot((rows * gain).astype(BF16), wq[layer, 0:columns])[0:8]
+        q = [q[:, 128 * g : 128 * g + 128] for g in range(4)]
+        q = jnp.concatenate([twice(q[0:2]), twice(q[2:4])], axis=0).astype(BF16)
+        rl_s[layer] = q
+        rl_r[layer, slot] = q
+
+    loads[2].wait()
+    loads[6].wait()
+    long_message(0, long_first, 128, me)
+
+    pl.semaphore_wait(barrier, len(peers) + len(strangers) + 2 * len(z_far))
 
     def remote(src, dst, send, recv, req, kv):
         return pltpu.make_async_remote_copy(
@@ -212,7 +231,20 @@
     for copy in shares:
         copy.start()
 
-    for at in (2, 3, 4, 6, 7, 8):
+    def send_long(layer, slot, everyone):
+        for req in everyone:
+            for src, dst, phase in (
+                (rl_s.at[layer], rl_r.at[layer, slot], RL),
+                (sl_s.at[layer], sl_r.at[layer, slot], SL),
+            ):
+                remote(
+                    src, dst, send_sem.at[layer, phase], recv_sem.at[layer, phase], req, my_z
+                ).start()
+
+    send_long(0, me, peers + strangers)
+    long_slots = (2 * n_chip, n_chip)
+
+    for at in (3, 4, 7, 8):
         loads[at].wait()
     shares[0].wait_recv()
     shares[1].wait_recv()
@@ -244,9 +276,6 @@
         copy.start()
         return copy
 
-    def as_row(column, mask):
-        return jnp.sum(jnp.where(mask, column, 0.0), axis=0, keepdims=True)
-
     def softmax_mean(s, v):
         top = jnp.maximum(jnp.max(s, axis=1, keepdims=True), CEIL)
         p = jnp.exp(s - top)
@@ -259,29 +288,8 @@
     others = pl.ds(0, n_chip - 1)
     on_diagonal = iota((half, 128), 0) == iota((half, 128), 1)
 
-    def send_long(layer, long_x):
-        square = jnp.sum(long_x * long_x, axis=1, keepdims=True)
-        square_row = as_row(square, row16 == lane16)
-        sl_s[layer] = square_row
-        sl_r[layer, chip] = square_row
-        gain = gains[pl.ds(layer, 1), :].astype(F32)
-        q = dot((long_x * gain).astype(BF16), wq[layer])[0:8]
-        q = [q[:, 128 * g : 128 * g + 128] for g in range(4)]
-        q = jnp.concatenate([twice(q[0:2]), twice(q[2:4])], axis=0).astype(BF16)
-        rl_s[layer] = q
-        rl_r[layer, chip] = q
-        to_chips(
-            lambda to: [
-                (rl_s.at[layer], rl_r.at[layer, chip], RL),
-                (sl_s.at[layer], sl_r.at[layer, chip], SL),
-            ],
-            layer,
-        )
-
     for layer in range(LAYERS):
         x = x_half[layer].reshape(half, 256)
-        if layer == 0:
-            send_long(layer, long_x)
         x = x.astype(F32)
         square = jnp.sum(x * x, axis=1, keepdims=True)
         square_row = as_row(square, on_diagonal)
@@ -332,14 +340,16 @@
             loads[15].wait()
 
         q_gain_row = q_gains[pl.ds(layer, 1), :].astype(F32)
-        arrived(sl_r.at[layer, others], recv_sem.at[layer, SL])
-        arrived(rl_r.at[layer, others], recv_sem.at[layer, RL])
+        slots = long_slots[layer]
+        arrived(sl_r.at[layer, pl.ds(0, slots - 1)], recv_sem.at[layer, SL])
+        arrived(rl_r.at[layer, pl.ds(0, slots - 1)], recv_sem.at[layer, RL])
         scale = lax.rsqrt(
-            jnp.sum(long_pick * jnp.sum(sl_r[layer], axis=0), axis=1, keepdims=True) / width
+            jnp.sum(long_pick * jnp.sum(sl_r[layer, 0:slots], axis=0), axis=1, keepdims=True)
+            / width
             + EPS
         )
         q_long = normed_turned(
-            jnp.sum(rl_r[layer].astype(F32), axis=0) * scale,
+            jnp.sum(rl_r[layer, 0:slots].astype(F32), axis=0) * scale,
             q_gain_row,
             long_cos[...],
             long_sin[...],
@@ -503,7 +513,8 @@
             long_x = long_x + jnp.concatenate([gained, jnp.zeros((8, 256), F32)], axis=0)
             for at in (6, 7, 8):
                 shares[at].wait_recv()
-            send_long(layer + 1, long_x.astype(BF16).astype(F32))
+            long_message(layer + 1, long_x.astype(BF16).astype(F32), 256, chip)
+            send_long(layer + 1, chip, peers)
             if owners > 1:
                 arrived(x_half.at[layer + 1, pl.ds(0, owners - 1)], recv_sem.at[layer, ZA])
         else:
@@ -539,8 +550,8 @@
         for ref, phase in (
             (rs_r.at[layer, others], RS),
             (sq_r.at[layer, others], SQ),
-            (rl_r.at[layer, others], RL),
-            (sl_r.at[layer, others], SL),
+            (rl_r.at[layer, pl.ds(0, long_slots[layer] - 1)], RL),
+            (sl_r.at[layer, pl.ds(0, long_slots[layer] - 1)], SL),
             (px_r.at[layer], PX),
             (ho_r.at[layer, others], HO),
             (ll_r.at[layer, others], LL),
@@ -626,9 +637,9 @@
             vmem((LAYERS, 1, 128), F32),
             vmem((*both, 1, 128), F32),
             vmem((LAYERS, 16, 128), BF16),
-            vmem((*both, 16, 128), BF16),
+            vmem((LAYERS, 2 * n_chip, 16, 128), BF16),
             vmem((LAYERS, 1, 128), F32),
-            vmem((*both, 1, 128), F32),
+            vmem((LAYERS, 2 * n_chip, 1, 128), F32),
             vmem((8, 128), BF16),
             vmem((2, nz, 8, 128), BF16),
             vmem((LAYERS, 32, 128), F32),

time: 56.8 us -> 55.8 us (0.982)
  Pallas kernels: 56 us -> 55.1 us
    pallas_call x1, Pallas kernels: 55.4 us -> 54.4 us  [on_device(): pl.pallas_call(functools.partial(kernel, n_chip, side, nz, float(width)),...]
where the time goes in v7:
time: 55.8 us; the launch traced here: 55.7 us
  Pallas kernels  55.1 us (99%)
  between operations  0.64 us (1%)
    pallas_call x1, Pallas kernels, on_device(): pl.pallas_call(functools.partial(kernel, n_chip, side, nz, float(width)),...  54.4 us

profile of v7, /device:TPU:1, one launch (start us, length us, event | category | flops | bytes accessed | tf_op | source)
XLA Modules:
  0.0 55.7 jit_solution(6367271098383500235)
XLA Ops:
  0.6 54.4 %attention_layers.1 = (bf16[2,128,128]{2,1,0:T(8,128)(2,1)S(1)}, bf16[2,8,128]{2,1,0:T(8,128)(2,1)S(1)}, bf16[2,8,128]{2,1,0:T(8,128)(2,1)S(1)}) custom-call(bf16[256,128]{1,0:T(8,128)(2,1)} %x_in.1, bf16[2,128]{1,0:T(2,128)(2,1)} %norm_gain.1, bf16[2,128]{1,0:T(2,128)(2,1)} %q_gain.1, bf16[2,128]{1,0:T(2,128)(2,1)} %k_gain.1, bf16[2,128,512]{2,1,0:T(8,128)(2,1)} %w_query.1, ...), custom_call_target="tpu_custom_call" | custom-call | tf_op jit(solution)/shard_map/attention_layers/pallas_call | solution.py:604
  55.0 0.7 %finish.1 = (bf16[16,2,8,128]{3,2,1,0:T(8,128)(2,1)}, bf16[2,8,128]{2,1,0:T(8,128)(2,1)}, bf16[2,8,128]{2,1,0:T(8,128)(2,1)}) custom-call(bf16[2,16,8,128]{3,2,1,0:T(8,128)(2,1)S(1)} %bitcast.3, bf16[2,8,128]{2,1,0:T(8,128)(2,1)S(1)} %get-tuple-element.10.new_keys, bf16[2,8,128]{2,1,0:T(8,128)(2,1)S(1)} %get-tuple-element.11.new_values), custom_call_target="tpu_custom_call" | custom-call | tf_op jit(solution)/shard_map/finish/pallas_call | solution.py:669

commit v8 on v7

--- a/solution.py
+++ b/solution.py
@@ -67,7 +67,10 @@
 
     steps = sorted(
         [(dx, dy) for dx in range(side) for dy in range(side) if dx or dy],
-        key=lambda d: -ring(d[0], side) - ring(d[1], side),
+        key=lambda d: (
+            -ring(d[0], side) - ring(d[1], side),
+            -max(ring(d[0], side), ring(d[1], side)),
+        ),
     )
     at_x = [lax.rem(chip_x + d, side) * side for d in range(side)]
     at_y = [lax.rem(chip_y + d, side) for d in range(side)]
@@ -195,8 +198,8 @@
         rl_s[layer] = q
         rl_r[layer, slot] = q
 
-    loads[2].wait()
-    loads[6].wait()
+    for at in (2, 6, 7, 8):
+        loads[at].wait()
     long_message(0, long_first, 128, me)
 
     pl.semaphore_wait(barrier, len(peers) + len(strangers) + 2 * len(z_far))
@@ -215,11 +218,11 @@
         remote(src, dst, init_send.at[at], init_recv.at[at], sib, my_z)
         for at, (src, dst) in enumerate(
             [
-                (x_in, x_sib),
-                (norm_gain, gains.at[:, pl.ds(128, 128)]),
-                (w_query.at[0], wq.at[0, pl.ds(128, 128)]),
-                (w_key.at[0], wk.at[0, pl.ds(128, 128)]),
-                (w_value.at[0], wv.at[0, pl.ds(128, 128)]),
+                (x_own, x_sib),
+                (gains.at[:, pl.ds(0, 128)], gains.at[:, pl.ds(128, 128)]),
+                (wq.at[0, pl.ds(0, 128)], wq.at[0, pl.ds(128, 128)]),
+                (wk.at[0, pl.ds(0, 128)], wk.at[0, pl.ds(128, 128)]),
+                (wv.at[0, pl.ds(0, 128)], wv.at[0, pl.ds(128, 128)]),
                 (w_out.at[0], wo.at[0, 1]),
                 (w_query.at[1], wq.at[1, pl.ds(128, 128)]),
                 (w_key.at[1], wk.at[1, pl.ds(128, 128)]),
@@ -228,7 +231,7 @@
             ]
         )
     ]
-    for copy in shares:
+    for copy in shares[:5]:
         copy.start()
 
     def send_long(layer, slot, everyone):
@@ -241,10 +244,11 @@
                     src, dst, send_sem.at[layer, phase], recv_sem.at[layer, phase], req, my_z
                 ).start()
 
-    send_long(0, me, peers + strangers)
+    in_turn = [req for pair in zip(peers, strangers) for req in pair] + [sib]
+    send_long(0, me, in_turn)
     long_slots = (2 * n_chip, n_chip)
 
-    for at in (3, 4, 7, 8):
+    for at in (3, 4):
         loads[at].wait()
     shares[0].wait_recv()
     shares[1].wait_recv()
@@ -312,6 +316,9 @@
         rs_r[layer, chip] = rs_s[layer, chip]
 
         if layer == 0:
+            for copy in shares[5:]:
+                copy.start()
+
             loads[9].wait()
             loads[10].wait()
 

time: 55.8 us -> 55.7 us (level)
  no operation moved by 1% of the time
where the time goes in v8:
time: 55.7 us
  Pallas kernels  55 us (99%)
  between operations  0.64 us (1%)
    pallas_call x1, Pallas kernels, on_device(): pl.pallas_call(functools.partial(kernel, n_chip, side, nz, float(width)),...  54.3 us

profile of v8, /device:TPU:1, one launch (start us, length us, event | category | flops | bytes accessed | tf_op | source)
XLA Modules:
  0.0 55.7 jit_solution(7989890238766486808)
XLA Ops:
  0.6 54.3 %attention_layers.1 = (bf16[2,128,128]{2,1,0:T(8,128)(2,1)S(1)}, bf16[2,8,128]{2,1,0:T(8,128)(2,1)S(1)}, bf16[2,8,128]{2,1,0:T(8,128)(2,1)S(1)}) custom-call(bf16[256,128]{1,0:T(8,128)(2,1)} %x_in.1, bf16[2,128]{1,0:T(2,128)(2,1)} %norm_gain.1, bf16[2,128]{1,0:T(2,128)(2,1)} %q_gain.1, bf16[2,128]{1,0:T(2,128)(2,1)} %k_gain.1, bf16[2,128,512]{2,1,0:T(8,128)(2,1)} %w_query.1, ...), custom_call_target="tpu_custom_call" | custom-call | tf_op jit(solution)/shard_map/attention_layers/pallas_call | solution.py:611
  55.0 0.7 %finish.1 = (bf16[16,2,8,128]{3,2,1,0:T(8,128)(2,1)}, bf16[2,8,128]{2,1,0:T(8,128)(2,1)}, bf16[2,8,128]{2,1,0:T(8,128)(2,1)}) custom-call(bf16[2,16,8,128]{3,2,1,0:T(8,128)(2,1)S(1)} %bitcast.3, bf16[2,8,128]{2,1,0:T(8,128)(2,1)S(1)} %get-tuple-element.10.new_keys, bf16[2,8,128]{2,1,0:T(8,128)(2,1)S(1)} %get-tuple-element.11.new_values), custom_call_target="tpu_custom_call" | custom-call | tf_op jit(solution)/shard_map/finish/pallas_call | solution.py:676
